TPU v7x, 128 devices: a whole 4x4x4 slice. The times are simulated.
128 devices in a mesh: row: 4 (over x), col: 32 (over z, y, core).
Axes of the slice: x: 4, y: 4, z: 4, core: 2. Of those that a mesh axis runs over, the one named last changes fastest.
Arguments:
- amplitudes: float32 [1024, 16384], P(None, ('row', 'col')), may hold values from -6 to 6
- integrals: float32 [16384, 16384], P('row', 'col'), may hold values from -0.078125 to 0.078125
- vv_coupling: float32 [128, 128], replicated, may hold values from -0.5 to 0.5
- amp_mask: int32 [32, 128], replicated, may hold values 0 or 1
- integral_mask: int32 [128, 128], replicated, may hold values from 0 to 1, as said below
Outputs:
- residual: float32 [32, 32, 128, 128], P('row', 'col')
Inputs may be any that keep to these rules, and one draw needn't show every extreme that they name: `amp_mask`: 1 keeps the amplitude tile (i, c), 0 screens it out. `integral_mask`: 1 keeps the integral tile (c, a), 0 screens it out.
All inputs are finite; a program needn't handle non-finite values.
Results may differ from a plain program's by a relative error of at most 0.00007.
Values sent between devices are 32-bit elements; how exact they have to be, the bound alone decides.
A program may use at most 192 MiB of HBM per device.

v0:
```python
import jax
import jax.numpy as jnp
from jax import lax
from jax.sharding import PartitionSpec as P


def body(amplitudes, integrals, vv_coupling, amp_mask, integral_mask):
    n_row = lax.axis_size("row")
    n_col = lax.axis_size("col")
    row_id = lax.axis_index("row")
    col_id = lax.axis_index("col")
    virt = vv_coupling.shape[0]
    pairs, k_local = amplitudes.shape
    occ_i = amp_mask.shape[0]
    occ_j = pairs // occ_i
    device_id = row_id * n_col + col_id
    col_index = device_id * k_local + jnp.arange(k_local, dtype=jnp.int32)
    tile_of_col = col_index // virt
    onehot = (tile_of_col[None, :] == jnp.arange(virt, dtype=jnp.int32)[:, None]).astype(
        jnp.float32
    )
    amp_cols = jnp.dot(amp_mask.astype(jnp.float32), onehot, precision=lax.Precision.HIGHEST)
    amp_screened = (amplitudes.reshape(occ_i, occ_j, k_local) * amp_cols[:, None, :]).reshape(
        pairs, k_local
    )
    c_rows = virt // n_row
    a_cols = virt // n_col
    mask_local = lax.dynamic_slice(
        integral_mask, (row_id * c_rows, col_id * a_cols), (c_rows, a_cols)
    )
    ints_kept = (
        integrals.reshape(c_rows, virt, a_cols, virt)
        * mask_local.astype(jnp.float32)[:, None, :, None]
    )
    k_row_len = c_rows * virt
    n_local = a_cols * virt
    ints_kept = ints_kept.reshape(k_row_len, n_local)
    p_rows = pairs // n_row
    own_rows = lax.all_to_all(amp_screened, "row", split_axis=0, concat_axis=1, tiled=True)
    ints_full = lax.all_gather(ints_kept, "row", axis=0, tiled=True)
    ints_order = (
        ints_full.reshape(n_row, n_col, k_local, n_local)
        .transpose(1, 0, 2, 3)
        .reshape(n_row * n_col * k_local, n_local)
    )
    ladder = jnp.dot(
        lax.all_gather(own_rows, "col", axis=1, tiled=True),
        ints_order,
        precision=lax.Precision.HIGHEST,
    )
    i_local = p_rows // occ_j
    blocks = ladder.reshape(i_local, occ_j, a_cols, virt)
    block = lax.all_to_all(blocks, "col", split_axis=1, concat_axis=2, tiled=True)
    return block + jnp.einsum("ac,ijcb->ijab", vv_coupling, block, precision=lax.Precision.HIGHEST)


def solution(mesh):
    in_specs = (P(None, ("row", "col")), P("row", "col"), P(), P(), P())
    out_specs = P("row", "col", None, None)
    return jax.shard_map(body, mesh=mesh, in_specs=in_specs, out_specs=out_specs, check_vma=False)
```

profile of v0, /device:TPU:1, one launch (start us, length us, event | category | flops | bytes accessed | tf_op | source)
XLA Modules:
  0.0 461.7 jit_solution(13501797368170229616)
XLA Ops:
  6.5 0.0 copy-start
  6.5 0.0 all-gather.5.cloned.1.call-start
  6.5 0.8 dynamic-slice_convert_fusion
  7.4 4.4 mul.38
  11.7 0.0 copy-start.2
  11.7 0.0 copy-start.1
  11.7 11.1 %bitcast_multiply_fusion = f32[4096,512]{1,0:T(8,128)} fusion(f32[4096,512]{1,0:T(8,128)} %param.6, f32[512,8,4,128]{3,2,1,0:T(4,128)} %bitcast.43), kind=kLoop, calls=%fused_computation | loop fusion | flops 2097152 | bytes 25165824 | tf_op jit(solution)/shard_map/mul | solution.py:32
  22.9 0.0 all-gather.5.cloned.1.call-update
  22.9 0.0 all-gather.3.cloned.1.call-start
  23.0 0.0 copy-done.2
  23.0 0.1 convolution_bitcast_fusion.1
  23.1 0.0 copy-done.1
  23.1 0.1 bitcast_multiply_fusion.1
  23.2 13.3 %all_to_all.31 = f32[4,256,128]{2,1,0:T(8,128)S(1)} all-to-all(f32[4,256,128]{2,1,0:T(8,128)S(1)} %bitcast.48), channel_id=1, replica_groups=mesh['row'=4,'col'=32] {'row'}, dimensions={0} | all-to-all | bytes 1048576 | tf_op jit(solution)/shard_map/all_to_all | solution.py:39
  36.4 0.9 copy_bitcast_fusion
  37.3 0.0 all-gather.3.cloned.1.call-update
  37.3 282.6 %all-gather.5.cloned.1.call-done = f32[16384,512]{1,0:T(8,128)} async-done(((f32[4096,512]{1,0:T(8,128)}), f32[16384,512]{1,0:T(8,128)}) %all-gather.5.cloned.1.call-update) | async-done | bytes 33554448 | tf_op jit(solution)/shard_map/all_gather | solution.py:40
  319.9 40.1 %copy.17 = f32[32,4,128,512]{2,1,0,3:T(4,128)} copy(f32[32,4,128,512]{3,2,0,1:T(8,128)} %bitcast.44) | data formatting | bytes 67108864 | tf_op jit(solution)/shard_map/transpose | solution.py:43
  360.0 40.4 %reshape.48 = f32[16384,512]{0,1:T(8,128)} reshape(f32[32,4,128,512]{2,1,0,3:T(4,128)} %copy.17) | data formatting | bytes 67108864 | tf_op jit(solution)/shard_map/reshape | solution.py:44
  400.4 0.0 all-gather.3.cloned.1.call-done
  400.4 32.6 %fusion.5 = f32[8,32,4,128]{3,1,2,0:T(8,128)S(1)} fusion(f32[8,32,16384,1]{2,1,3,0:T(8,128)} %bitcast.49, f32[4,128,16384,1]{2,1,0,3:T(8,128)} %bitcast.45), kind=kOutput, calls=%fused_computation.16 | convolution fusion | flops 25769803776 | bytes 50855936 | tf_op jit(solution)/shard_map/dot_general | solution.py:46
  433.0 0.3 copy.18
  433.3 19.2 %all_to_all.32 = f32[8,32,4,128]{3,2,0,1:T(4,128)S(1)} all-to-all(f32[8,32,4,128]{3,2,0,1:T(4,128)S(1)} %copy.18), channel_id=1, replica_groups=mesh['row'=4,'col'=32] {'col'}, dimensions={1} | all-to-all | bytes 1048576 | tf_op jit(solution)/shard_map/all_to_all | solution.py:53
  452.6 0.2 copy.22
  452.8 0.0 copy-done
  452.8 1.0 fusion
  453.8 1.0 copy.23
  (2 shorter events, 0.0 us)
Async XLA Ops:
  6.5 446.3 %copy-start = (f32[128,128]{1,0:T(8,128)S(1)}, f32[128,128]{1,0:T(8,128)}, u32[]{:S(2)}) copy-start(f32[128,128]{1,0:T(8,128)} %param.7) | copy-start | bytes 196612
  6.5 313.4 %all-gather.5.cloned.1.call-start = ((), (), s32[]{:S(2)}) async-start(), calls=%async_computation.3 | async-start | bytes 41943040 | tf_op jit(solution)/shard_map/all_gather | solution.py:40
  11.7 11.2 %copy-start.2 = (s32[32,128]{1,0:T(8,128)S(1)}, s32[32,128]{1,0:T(8,128)}, u32[]{:S(2)}) copy-start(s32[32,128]{1,0:T(8,128)} %param.8) | copy-start | bytes 49156
  11.7 11.4 %copy-start.1 = (f32[1024,128]{1,0:T(8,128)S(1)}, f32[1024,128]{1,0:T(8,128)}, u32[]{:S(2)}) copy-start(f32[1024,128]{1,0:T(8,128)} %param.5) | copy-start | bytes 1572868
  22.9 377.5 %all-gather.3.cloned.1.call-start = ((), (), s32[]{:S(2)}) async-start(), calls=%async_computation.2 | async-start | bytes 17301504 | tf_op jit(solution)/shard_map/all_gather | solution.py:47
Sparse Core Ops, SparseCore 0:
  23.0 296.8 all-gather.4
  322.2 74.2 all-gather.2
where the time goes:
time: 464 us; the launch traced here: 462 us
  waiting for transfers between devices  283 us (61%)
  local copies, waits for them, and re-layouts  87.4 us (19%)
  matrix products  33.7 us (7%)
  blocking collectives  32.5 us (7%)
  between operations  13.5 us (3%)
  other arithmetic  12 us (3%)
    all_gather x1, waiting for transfers between devices, body(): ints_full = lax.all_gather(ints_kept, 'row', axis=0, tiled=True)  283 us
    reshape x1, local copies, waits for them, and re-layouts, body(): ints_order = ints_full.reshape(n_row, n_col, k_local, n_local).transpose(...  40.4 us
    transpose x1, local copies, waits for them, and re-layouts, body(): ints_order = ints_full.reshape(n_row, n_col, k_local, n_local).transpose(...  40.1 us
    dot_general x1, matrix products, body(): jnp.dot(lax.all_gather(own_rows, 'col', axis=1, tiled=True), ints_order,...  32.6 us
    all_to_all x1, blocking collectives, body(): lax.all_to_all(blocks, 'col', split_axis=1, concat_axis=2, tiled=True)  19.2 us
    all_to_all x1, blocking collectives, body(): lax.all_to_all(amp_screened, 'row', split_axis=0, concat_axis=1, tiled=True)  13.3 us
    mul x1, other arithmetic, body(): integrals.reshape(c_rows, virt, a_cols, virt)  11.1 us
  transfers between devices with their start and end apart: 2, of which 1 were waited for; matrix products, arithmetic and copies ran while one was open for 18% of the time, Pallas kernels for 0%

commit v1 on v0

v1 whole, which is shorter than its diff:
```python
import jax
import jax.numpy as jnp
from jax import lax
from jax.sharding import Mesh
from jax.sharding import PartitionSpec as P

COL = ("zy", "core")


def body(amplitudes, integrals, vv_coupling, amp_mask, integral_mask):
    n_row = lax.axis_size("row")
    n_zy = lax.axis_size("zy")
    n_core = lax.axis_size("core")
    n_col = n_zy * n_core
    row_id = lax.axis_index("row")
    core_id = lax.axis_index("core")
    col_id = lax.axis_index("zy") * n_core + core_id
    virt = vv_coupling.shape[0]
    pairs, k_local = amplitudes.shape
    occ_i = amp_mask.shape[0]
    occ_j = pairs // occ_i

    c_own = row_id * n_col + col_id
    amp_col = lax.dynamic_slice_in_dim(amp_mask, c_own, 1, axis=1).astype(jnp.float32)
    amp_screened = (amplitudes.reshape(occ_i, occ_j, k_local) * amp_col[:, :, None]).reshape(
        pairs, k_local
    )

    c_rows = virt // n_row
    a_cols = virt // n_col
    n_local = a_cols * virt
    mask_local = lax.dynamic_slice(
        integral_mask, (row_id * c_rows, col_id * a_cols), (c_rows, a_cols)
    ).astype(jnp.float32)
    ints = integrals.reshape(n_zy, n_core, k_local, a_cols, virt) * mask_local.reshape(
        n_zy, n_core, 1, a_cols, 1
    )
    ints = ints.transpose(1, 0, 2, 3, 4).reshape(n_core, n_zy * k_local, n_local)

    own = lax.all_gather(amp_screened, "zy", axis=1, tiled=True)
    other = lax.ppermute(own, "core", [(0, 1), (1, 0)])
    ints_own = lax.dynamic_index_in_dim(ints, core_id, 0, keepdims=False)
    ints_other = lax.dynamic_index_in_dim(ints, 1 - core_id, 0, keepdims=False)
    partial = jnp.dot(own, ints_own, precision=lax.Precision.HIGHEST) + jnp.dot(
        other, ints_other, precision=lax.Precision.HIGHEST
    )

    ladder = lax.psum_scatter(partial, "row", scatter_dimension=0, tiled=True)
    i_local = pairs // n_row // occ_j
    blocks = ladder.reshape(i_local, occ_j, a_cols, virt)
    block = lax.all_to_all(blocks, COL, split_axis=1, concat_axis=2, tiled=True)
    return block + jnp.einsum("ac,ijcb->ijab", vv_coupling, block, precision=lax.Precision.HIGHEST)


def solution(mesh):
    n_row, n_col = mesh.devices.shape
    mesh3 = Mesh(mesh.devices.reshape(n_row, n_col // 2, 2), ("row",) + COL)
    in_specs = (P(None, ("row",) + COL), P("row", COL), P(), P(), P())
    out_specs = P("row", COL, None, None)
    return jax.shard_map(body, mesh=mesh3, in_specs=in_specs, out_specs=out_specs, check_vma=False)
```

time: 464 us -> 219 us (0.47)
  waiting for transfers between devices: 283 us -> 108 us
  local copies, waits for them, and re-layouts: 87.4 us -> 30.1 us
  blocking collectives: 32.5 us -> 19 us
    all_gather x2 -> x1, waiting for transfers between devices: 283 us -> 79.3 us  [body(): own = lax.all_gather(amp_screened, 'zy', axis=1, tiled=True)]
    transpose x1 -> x0, local copies, waits for them, and re-layouts: 40.1 us -> none  [body(): ints_order = ints_full.reshape(n_row, n_col, k_local, n_local).transpose(...]
    reduce_scatter x0 -> x1, waiting for transfers between devices: none -> 28.5 us  [body(): ladder = lax.psum_scatter(partial, 'row', scatter_dimension=0, tiled=True)]
    all_to_all x2 -> x1, blocking collectives: 32.5 us -> 19 us  [body(): block = lax.all_to_all(blocks, COL, split_axis=1, concat_axis=2, tiled=True)]
    reshape x1 -> x5, local copies, waits for them, and re-layouts: 40.4 us -> 28.6 us  [the longest x2 17.8 us: body(): integrals.reshape(n_zy, n_core, k_local, a_cols, virt)]
    mul x2 -> x1, other arithmetic: 11.2 us -> 2.05 us  [body(): amplitudes.reshape(occ_i, occ_j, k_local) * amp_col[:, :, None]]
    transpose x0 -> x1, other arithmetic: none -> 7.54 us  [body(): ints.transpose(1, 0, 2, 3, 4).reshape(n_core, n_zy * k_local, n_local)]
  transfers between devices with their start and end apart: 2 -> 3, of which waited for: 1 -> 2; matrix products, arithmetic and copies ran while one was open for 18% -> 24% of each run, Pallas kernels for 0% -> 0%
where the time goes in v1:
time: 219 us
  waiting for transfers between devices  108 us (49%)
  matrix products  34.8 us (16%)
  local copies, waits for them, and re-layouts  30.1 us (14%)
  blocking collectives  19 us (9%)
  between operations  13.5 us (6%)
  other arithmetic  11.3 us (5%)
    all_gather x1, waiting for transfers between devices, body(): own = lax.all_gather(amp_screened, 'zy', axis=1, tiled=True)  79.3 us
    reduce_scatter x1, waiting for transfers between devices, body(): ladder = lax.psum_scatter(partial, 'row', scatter_dimension=0, tiled=True)  28.5 us
    all_to_all x1, blocking collectives, body(): block = lax.all_to_all(blocks, COL, split_axis=1, concat_axis=2, tiled=True)  19 us
    reshape x2, local copies, waits for them, and re-layouts, body(): integrals.reshape(n_zy, n_core, k_local, a_cols, virt)  17.8 us
    dot_general x1, matrix products, body(): jnp.dot(other, ints_other, precision=lax.Precision.HIGHEST)  17.3 us
    dot_general x1, matrix products, body(): jnp.dot(own, ints_own, precision=lax.Precision.HIGHEST)  16.5 us
    reshape x1, local copies, waits for them, and re-layouts, body(): ints.transpose(1, 0, 2, 3, 4).reshape(n_core, n_zy * k_local, n_local)  9.28 us
    transpose x1, other arithmetic, body(): ints.transpose(1, 0, 2, 3, 4).reshape(n_core, n_zy * k_local, n_local)  7.54 us
  transfers between devices with their start and end apart: 3, of which 2 were waited for; matrix products, arithmetic and copies ran while one was open for 24% of the time, Pallas kernels for 0%

profile of v1, /device:TPU:1, one launch (start us, length us, event | category | flops | bytes accessed | tf_op | source)
XLA Modules:
  0.0 218.5 jit_solution(3347700047959985236)
XLA Ops:
  6.5 0.0 copy-start
  6.5 0.0 all-gather.2.cloned.1.call-start
  6.5 0.9 convert_reduce_fusion
  7.5 0.1 mul.38
  7.5 0.1 mul.39
  7.6 2.0 broadcast_multiply_fusion
  9.7 0.0 all-gather.2.cloned.1.call-update
  9.7 0.0 reduce-scatter.2.cloned.1.call-start
  9.7 79.3 %all-gather.2.cloned.1.call-done = f32[1024,2048]{1,0:T(8,128)} async-done(((f32[1024,128]{1,0:T(8,128)}), f32[1024,2048]{1,0:T(8,128)}) %all-gather.2.cloned.1.call-update) | async-done | bytes 8388624 | tf_op jit(solution)/shard_map/all_gather | solution.py:40
  89.1 2.0 collective-permute-start
  91.1 0.8 dynamic-slice_convert_fusion
  91.9 0.1 copy.9
  92.0 9.9 %reshape.23 = f32[16,2,128,4,128]{4,3,2,1,0:T(4,128)} reshape(f32[4096,512]{1,0:T(8,128)} %param.6) | data formatting | bytes 16777216 | tf_op jit(solution)/shard_map/reshape | solution.py:35
  101.9 7.9 %copy.10 = f32[16,2,128,4,128]{2,0,4,3,1:T(8,128)} copy(f32[16,2,128,4,128]{4,3,2,1,0:T(4,128)} %reshape.23) | data formatting | bytes 16777216 | tf_op jit(solution)/shard_map/reshape | solution.py:35
  109.8 7.5 %multiply_bitcast_fusion = f32[2,16,128,4,128]{2,1,4,3,0:T(8,128)} fusion(f32[16,2,128,4,128]{2,0,4,3,1:T(8,128)} %copy.10, f32[16,2,4]{0,2,1:T(4,128)S(1)} %copy.9), kind=kLoop, calls=%fused_computation | loop fusion | flops 2097152 | bytes 16777728 | tf_op jit(solution)/shard_map/transpose | solution.py:38
  117.4 9.3 %reshape.24 = f32[2,2048,512]{1,2,0:T(8,128)} reshape(f32[2,16,128,4,128]{2,1,4,3,0:T(8,128)} %multiply_bitcast_fusion) | data formatting | bytes 16777216 | tf_op jit(solution)/shard_map/reshape | solution.py:38
  126.6 0.0 copy-start.1
  126.6 16.5 %fusion.2 = f32[1024,512]{1,0:T(8,128)S(1)} fusion(f32[1024,2048]{1,0:T(8,128)} %all-gather.2.cloned.1.call-done, f32[2,2048,512]{1,2,0:T(8,128)} %reshape.24, s32[]{:T(128)S(6)} %select_n.19), kind=kOutput, calls=%fused_computation.3 | convolution fusion | flops 12884901888 | bytes 14680068 | tf_op jit(solution)/shard_map/dot_general | solution.py:44
  143.1 0.0 collective-permute-done
  143.1 0.0 copy-done.1
  143.1 17.3 %fusion.6 = f32[1024,512]{1,0:T(8,128)} fusion(f32[1024,512]{1,0:T(8,128)S(1)} %fusion.2, f32[1024,2048]{1,0:T(8,128)} %collective-permute-done, f32[2,2048,512]{1,2,0:T(8,128)S(1)} %copy-done.1, s32[]{:T(128)S(6)} %select_n.20), kind=kOutput, calls=%fused_computation.7 | convolution fusion | flops 12885426176 | bytes 16777220 | tf_op jit(solution)/shard_map/dot_general | solution.py:44
  160.4 0.0 reduce-scatter.2.cloned.1.call-update
  160.4 28.5 %reduce-scatter.2.cloned.1.call-done = f32[256,512]{1,0:T(8,128)} async-done(((f32[1024,512]{1,0:T(8,128)}), f32[256,512]{1,0:T(8,128)}) %reduce-scatter.2.cloned.1.call-update) | async-done | bytes 524304 | tf_op jit(solution)/shard_map/reduce_scatter | solution.py:48
  188.9 1.2 reshape.25
  190.1 0.3 copy.11
  190.4 19.0 %all_to_all.12 = f32[8,32,4,128]{3,0,2,1:T(8,128)S(1)} all-to-all(f32[8,32,4,128]{3,0,2,1:T(8,128)S(1)} %copy.11), channel_id=1, replica_groups=mesh['row'=4,'zy'=16,'core'=2] {'zy','core'}, dimensions={1} | all-to-all | bytes 1048576 | tf_op jit(solution)/shard_map/all_to_all | solution.py:51
  209.4 0.2 copy.13
  209.7 0.0 copy-done
  209.7 1.0 fusion.9
  210.7 1.0 copy.14
Async XLA Ops:
  6.5 203.1 %copy-start = (f32[128,128]{1,0:T(8,128)S(1)}, f32[128,128]{1,0:T(8,128)}, u32[]{:S(2)}) copy-start(f32[128,128]{1,0:T(8,128)} %param.7) | copy-start | bytes 196612
  6.5 82.5 %all-gather.2.cloned.1.call-start = ((), (), s32[]{:S(2)}) async-start(), calls=%async_computation.2 | async-start | bytes 8912896 | tf_op jit(solution)/shard_map/all_gather | solution.py:40
  9.7 179.2 %reduce-scatter.2.cloned.1.call-start = ((), (), s32[]{:S(2)}) async-start(), calls=%async_computation.3 | async-start | bytes 2621440 | tf_op jit(solution)/shard_map/reduce_scatter | solution.py:48
  89.1 54.1 %collective-permute-start = (f32[1024,2048]{1,0:T(8,128)}, f32[1024,2048]{1,0:T(8,128)}, u32[]{:S(2)}, u32[]{:S(2)}) collective-permute-start(f32[1024,2048]{1,0:T(8,128)} %all-gather.2.cloned.1.call-done), channel_id=1, source_target_pairs={{0,1},{1,0},{2,3},{3,2},{4,5},{5,4},{6,7},{7,6},{8,9},{9,8},{10,11... | collective-permute-start | bytes 25165832 | tf_op jit(solution)/shard_map/ppermute | solution.py:41
  126.6 16.5 %copy-start.1 = (f32[2,2048,512]{1,2,0:T(8,128)S(1)}, f32[2,2048,512]{1,2,0:T(8,128)}, u32[]{:S(2)}) copy-start(f32[2,2048,512]{1,2,0:T(8,128)} %reshape.24) | copy-start | bytes 25165828
Sparse Core Ops, SparseCore 0:
  9.8 79.2 all-gather.1
  160.6 28.3 reduce-scatter.1

commit v2 on v1

v2 whole, which is shorter than its diff:
```python
import jax
import jax.numpy as jnp
from jax import lax
from jax.sharding import Mesh
from jax.sharding import PartitionSpec as P

PLANE = ("z", "y")
COL = PLANE + ("core",)


def body(amplitudes, integrals, vv_coupling, amp_mask, integral_mask):
    n_row = lax.axis_size("row")
    n_zy = lax.axis_size(PLANE)
    n_core = lax.axis_size("core")
    n_col = n_zy * n_core
    row_id = lax.axis_index("row")
    core_id = lax.axis_index("core")
    col_id = lax.axis_index(PLANE) * n_core + core_id
    virt = vv_coupling.shape[0]
    pairs, k_local = amplitudes.shape
    occ_i = amp_mask.shape[0]
    occ_j = pairs // occ_i

    c_own = row_id * n_col + col_id
    amp_col = lax.dynamic_slice_in_dim(amp_mask, c_own, 1, axis=1).astype(jnp.float32)
    amp_screened = (amplitudes.reshape(occ_i, occ_j, k_local) * amp_col[:, :, None]).reshape(
        pairs, k_local
    )

    c_rows = virt // n_row
    a_cols = virt // n_col
    n_local = a_cols * virt
    mask_local = lax.dynamic_slice(
        integral_mask, (row_id * c_rows, col_id * a_cols), (c_rows, a_cols)
    ).astype(jnp.float32)
    mask_wide = jnp.repeat(mask_local, virt, axis=1)
    ints = integrals.reshape(n_zy, n_core, k_local, n_local) * mask_wide.reshape(
        n_zy, n_core, 1, n_local
    )

    own = lax.all_gather(amp_screened, PLANE, axis=1, tiled=True)
    other = lax.ppermute(own, "core", [(0, 1), (1, 0)])
    ints_own = lax.dynamic_index_in_dim(ints, core_id, 1, keepdims=False)
    ints_other = lax.dynamic_index_in_dim(ints, 1 - core_id, 1, keepdims=False)
    own = own.reshape(pairs, n_zy, k_local)
    other = other.reshape(pairs, n_zy, k_local)
    dims = (((1, 2), (0, 1)), ((), ()))
    partial = lax.dot_general(own, ints_own, dims, precision=lax.Precision.HIGH) + lax.dot_general(
        other, ints_other, dims, precision=lax.Precision.HIGH
    )

    ladder = lax.psum_scatter(partial, "row", scatter_dimension=0, tiled=True)
    i_local = pairs // n_row // occ_j
    blocks = ladder.reshape(i_local, occ_j, a_cols, virt)
    block = lax.all_to_all(blocks, COL, split_axis=1, concat_axis=2, tiled=True)
    return block + jnp.einsum("ac,ijcb->ijab", vv_coupling, block, precision=lax.Precision.HIGHEST)


def solution(mesh):
    n_row, n_col = mesh.devices.shape
    n_side = int(round((n_col // 2) ** 0.5))
    mesh3 = Mesh(mesh.devices.reshape(n_row, n_side, n_col // 2 // n_side, 2), ("row",) + COL)
    in_specs = (P(None, ("row",) + COL), P("row", COL), P(), P(), P())
    out_specs = P("row", COL, None, None)
    return jax.shard_map(body, mesh=mesh3, in_specs=in_specs, out_specs=out_specs, check_vma=False)
```

time: 219 us -> 168 us (0.77)
  local copies, waits for them, and re-layouts: 30.1 us -> 5.32 us
  matrix products: 34.8 us -> 18.7 us
  waiting for transfers between devices: 108 us -> 103 us
  other arithmetic: 11.3 us -> 7.3 us
    reshape x3 -> x0, local copies, waits for them, and re-layouts: 27.1 us -> none  [the longest x2 17.8 us: body(): integrals.reshape(n_zy, n_core, k_local, a_cols, virt)]
    dot_general x2, matrix products: 33.8 us -> 17.7 us  [the longest x1 10.8 us: body(): lax.dot_general(other, ints_other, dims, precision=lax.Precision.HIGH)]
    transpose x1 -> x0, other arithmetic: 7.54 us -> none  [body(): ints.transpose(1, 0, 2, 3, 4).reshape(n_core, n_zy * k_local, n_local)]
    all_gather x1, waiting for transfers between devices: 79.3 us -> 74.1 us  [body(): own = lax.all_gather(amp_screened, PLANE, axis=1, tiled=True)]
    mul x0 -> x1, other arithmetic: none -> 4.73 us  [body(): integrals.reshape(n_zy, n_core, k_local, n_local)]
    unnamed x4 -> x5, local copies, waits for them, and re-layouts: 0.01 us -> 2.27 us
  transfers between devices with their start and end apart: 3 -> 3, of which waited for: 2 -> 2; matrix products, arithmetic and copies ran while one was open for 24% -> 7% of each run, Pallas kernels for 0% -> 0%
where the time goes in v2:
time: 168 us
  waiting for transfers between devices  103 us (61%)
  blocking collectives  19 us (11%)
  matrix products  18.7 us (11%)
  between operations  13.5 us (8%)
  other arithmetic  7.3 us (4%)
  local copies, waits for them, and re-layouts  5.32 us (3%)
    all_gather x1, waiting for transfers between devices, body(): own = lax.all_gather(amp_screened, PLANE, axis=1, tiled=True)  74.1 us
    reduce_scatter x1, waiting for transfers between devices, body(): ladder = lax.psum_scatter(partial, 'row', scatter_dimension=0, tiled=True)  28.8 us
    all_to_all x1, blocking collectives, body(): block = lax.all_to_all(blocks, COL, split_axis=1, concat_axis=2, tiled=True)  19 us
    dot_general x1, matrix products, body(): lax.dot_general(other, ints_other, dims, precision=lax.Precision.HIGH)  10.8 us
    dot_general x1, matrix products, body(): lax.dot_general(own, ints_own, dims, precision=lax.Precision.HIGH)  6.88 us
    mul x1, other arithmetic, body(): integrals.reshape(n_zy, n_core, k_local, n_local)  4.73 us
  transfers between devices with their start and end apart: 3, of which 2 were waited for; matrix products, arithmetic and copies ran while one was open for 7% of the time, Pallas kernels for 0%

profile of v2, /device:TPU:1, one launch (start us, length us, event | category | flops | bytes accessed | tf_op | source)
XLA Modules:
  0.0 167.6 jit_solution(2194645711003968548)
XLA Ops:
  6.5 0.0 copy-start
  6.5 0.0 all-gather.2.cloned.1.call-start
  6.5 0.9 convert_reduce_fusion
  7.5 0.1 mul.42
  7.5 0.1 mul.43
  7.6 1.2 copy.10
  8.9 0.8 broadcast_multiply_fusion
  9.7 0.0 all-gather.2.cloned.1.call-update
  9.7 0.0 reduce-scatter.2.cloned.1.call-start
  9.8 74.1 %all-gather.2.cloned.1.call-done = f32[1024,2048]{0,1:T(8,128)} async-done(((f32[1024,128]{0,1:T(8,128)}), f32[1024,2048]{0,1:T(8,128)}) %all-gather.2.cloned.1.call-update) | async-done | bytes 8388624 | tf_op jit(solution)/shard_map/all_gather | solution.py:41
  83.9 0.8 collective-permute-start
  84.7 0.8 dynamic-slice_convert_fusion
  85.5 0.1 broadcast_in_dim.4
  85.6 0.1 mul.47
  85.7 0.0 copy-start.1
  85.7 4.7 %copy_multiply_fusion = f32[16,2,128,512]{3,2,0,1:T(8,128)S(1)} fusion(f32[16,2,128,512]{3,2,1,0:T(8,128)} %bitcast.28, f32[16,2,512]{2,0,1:T(8,128)S(1)} %copy.11), kind=kLoop, calls=%fused_computation | loop fusion | flops 2097152 | bytes 16842752 | tf_op jit(solution)/shard_map/mul | solution.py:37
  90.4 1.0 copy-done.1
  91.5 6.9 %fusion.2 = f32[1024,512,1]{1,0,2:T(8,128)S(1)} fusion(f32[1024,16,128]{0,2,1:T(8,128)S(1)} %bitcast.31, f32[16,2,128,512]{3,2,0,1:T(8,128)S(1)} %copy_multiply_fusion, s32[]{:T(128)S(6)} %select_n.19), kind=kOutput, calls=%fused_computation.3 | convolution fusion | flops 6442450944 | bytes 14680068 | tf_op jit(solution)/shard_map/dot_general | solution.py:48
  98.3 0.0 collective-permute-done
  98.4 10.8 %bitcast_add_fusion = f32[1024,512]{1,0:T(8,128)} fusion(f32[1024,512,1]{1,0,2:T(8,128)S(1)} %fusion.2, f32[1024,16,128]{0,2,1:T(8,128)} %bitcast.4, f32[16,2,128,512]{3,2,0,1:T(8,128)S(1)} %copy_multiply_fusion, s32[]{:T(128)S(6)} %select_n.20), kind=kOutput, calls=%fused_computation.7 | convolution fusion | flops 6442975232 | bytes 16777220 | tf_op jit(solution)/shard_map/dot_general | solution.py:48
  109.1 0.0 reduce-scatter.2.cloned.1.call-update
  109.2 28.8 %reduce-scatter.2.cloned.1.call-done = f32[256,512]{1,0:T(8,128)} async-done(((f32[1024,512]{1,0:T(8,128)}), f32[256,512]{1,0:T(8,128)}) %reduce-scatter.2.cloned.1.call-update) | async-done | bytes 524304 | tf_op jit(solution)/shard_map/reduce_scatter | solution.py:52
  138.0 1.2 reshape.28
  139.2 0.3 copy.15
  139.5 19.0 %all_to_all.12 = f32[8,32,4,128]{3,0,2,1:T(8,128)S(1)} all-to-all(f32[8,32,4,128]{3,0,2,1:T(8,128)S(1)} %copy.15), channel_id=1, replica_groups=mesh['row'=4,'z'=4,'y'=4,'core'=2] {'z','y','core'}, dimensions={1} | all-to-all | bytes 1048576 | tf_op jit(solution)/shard_map/all_to_all | solution.py:55
  158.5 0.2 copy.17
  158.7 0.0 copy-done
  158.7 1.0 fusion.8
  159.7 1.0 copy.18
  (1 shorter events, 0.0 us)
Async XLA Ops:
  6.5 152.2 %copy-start = (f32[128,128]{1,0:T(8,128)S(1)}, f32[128,128]{1,0:T(8,128)}, u32[]{:S(2)}) copy-start(f32[128,128]{1,0:T(8,128)} %param.7) | copy-start | bytes 196612
  6.5 77.3 %all-gather.2.cloned.1.call-start = ((), (), s32[]{:S(2)}) async-start(), calls=%async_computation.2 | async-start | bytes 8912896 | tf_op jit(solution)/shard_map/all_gather | solution.py:41
  9.7 128.2 %reduce-scatter.2.cloned.1.call-start = ((), (), s32[]{:S(2)}) async-start(), calls=%async_computation.3 | async-start | bytes 2621440 | tf_op jit(solution)/shard_map/reduce_scatter | solution.py:52
  83.9 14.5 %collective-permute-start = (f32[1024,2048]{0,1:T(8,128)}, f32[1024,2048]{0,1:T(8,128)}, u32[]{:S(2)}, u32[]{:S(2)}) collective-permute-start(f32[1024,2048]{0,1:T(8,128)} %all-gather.2.cloned.1.call-done), channel_id=1, source_target_pairs={{0,1},{1,0},{2,3},{3,2},{4,5},{5,4},{6,7},{7,6},{8,9},{9,8},{10,11... | collective-permute-start | bytes 25165832 | tf_op jit(solution)/shard_map/ppermute | solution.py:42
  85.7 5.8 %copy-start.1 = (f32[1024,2048]{0,1:T(8,128)S(1)}, f32[1024,2048]{0,1:T(8,128)}, u32[]{:S(2)}) copy-start(f32[1024,2048]{0,1:T(8,128)} %all-gather.2.cloned.1.call-done) | copy-start | bytes 25165828
Sparse Core Ops, SparseCore 0:
  9.9 73.9 all-gather.1
  109.3 28.6 reduce-scatter.1

commit v3 on v2

v3 whole, which is shorter than its diff:
```python
import jax
import jax.numpy as jnp
from jax import lax
from jax.sharding import Mesh
from jax.sharding import PartitionSpec as P

PLANE = ("z", "y")
COL = PLANE + ("core",)
N_CHUNKS = 2


def shift(x, axis, step):
    n = lax.axis_size(axis)
    return lax.ppermute(x, axis, [(p, (p + step) % n) for p in range(n)])


def ring_gather(block, axis):
    n = lax.axis_size(axis)
    ahead = [block]
    behind = []
    for _ in range((n - 1) // 2):
        ahead.append(shift(ahead[-1], axis, -1))
        behind.append(shift(behind[-1] if behind else block, axis, +1))
    if n % 2 == 0 and n > 1:
        half = block.shape[0] // 2
        src_a = ahead[-1]
        src_b = behind[-1] if behind else block
        far = jnp.concatenate([shift(src_a[:half], axis, -1), shift(src_b[half:], axis, +1)], 0)
        ahead.append(far)
    return jnp.concatenate(ahead + behind[::-1], axis=1)


def body(amplitudes, integrals, vv_coupling, amp_mask, integral_mask):
    n_row = lax.axis_size("row")
    n_z = lax.axis_size("z")
    n_y = lax.axis_size("y")
    n_core = lax.axis_size("core")
    n_col = n_z * n_y * n_core
    row_id = lax.axis_index("row")
    z_id = lax.axis_index("z")
    y_id = lax.axis_index("y")
    core_id = lax.axis_index("core")
    col_id = (z_id * n_y + y_id) * n_core + core_id
    virt = vv_coupling.shape[0]
    pairs, k_local = amplitudes.shape
    occ_i = amp_mask.shape[0]
    occ_j = pairs // occ_i

    c_own = row_id * n_col + col_id
    amp_col = lax.dynamic_slice_in_dim(amp_mask, c_own, 1, axis=1).astype(jnp.float32)
    amp_screened = (amplitudes.reshape(occ_i, occ_j, k_local) * amp_col[:, :, None]).reshape(
        pairs, k_local
    )

    c_rows = virt // n_row
    a_cols = virt // n_col
    n_local = a_cols * virt
    mask_local = lax.dynamic_slice(
        integral_mask, (row_id * c_rows, col_id * a_cols), (c_rows, a_cols)
    ).astype(jnp.float32)
    mask_wide = jnp.repeat(mask_local, virt, axis=1)
    ints = integrals.reshape(c_rows, k_local, n_local) * mask_wide[:, None, :]
    dc = jnp.arange(n_core, dtype=jnp.int32)[:, None, None]
    dz = jnp.arange(n_z, dtype=jnp.int32)[None, :, None]
    dy = jnp.arange(n_y, dtype=jnp.int32)[None, None, :]
    tile = (((z_id + dz) % n_z) * n_y + (y_id + dy) % n_y) * n_core + (core_id + dc) % n_core
    ints_rel = jnp.take(ints, tile.reshape(-1), axis=0).reshape(n_core, n_z * n_y * k_local, n_local)

    i_local = occ_i // n_row
    i_chunk = i_local // N_CHUNKS
    amp_chunks = amp_screened.reshape(n_row, N_CHUNKS, i_chunk * occ_j, k_local)
    outs = []
    for h in range(N_CHUNKS):
        a_h = amp_chunks[:, h].reshape(n_row * i_chunk * occ_j, k_local)
        own = ring_gather(ring_gather(a_h, "y"), "z")
        other = lax.ppermute(own, "core", [(0, 1), (1, 0)])
        partial = jnp.dot(own, ints_rel[0], precision=lax.Precision.HIGH) + jnp.dot(
            other, ints_rel[1], precision=lax.Precision.HIGH
        )
        ladder = lax.psum_scatter(partial, "row", scatter_dimension=0, tiled=True)
        blocks = ladder.reshape(i_chunk, occ_j, a_cols, virt)
        outs.append(lax.all_to_all(blocks, COL, split_axis=1, concat_axis=2, tiled=True))
    block = jnp.concatenate(outs, axis=0)
    return block + jnp.einsum("ac,ijcb->ijab", vv_coupling, block, precision=lax.Precision.HIGHEST)


def solution(mesh):
    n_row, n_col = mesh.devices.shape
    n_side = int(round((n_col // 2) ** 0.5))
    mesh4 = Mesh(mesh.devices.reshape(n_row, n_side, n_col // 2 // n_side, 2), ("row",) + COL)
    in_specs = (P(None, ("row",) + COL), P("row", COL), P(), P(), P())
    out_specs = P("row", COL, None, None)
    return jax.shard_map(body, mesh=mesh4, in_specs=in_specs, out_specs=out_specs, check_vma=False)
```

time: 168 us -> 227 us (1.35)
  starting transfers between devices: 0.88 us -> 46.2 us
  local copies, waits for them, and re-layouts: 5.32 us -> 26.4 us
  blocking collectives: 19 us -> 0 us
  other arithmetic: 7.3 us -> 19.4 us
  waiting for transfers between devices: 103 us -> 91.1 us
  matrix products: 18.7 us -> 29.3 us
    all_gather x1 -> x0, waiting for transfers between devices: 74.1 us -> none  [body(): own = lax.all_gather(amp_screened, PLANE, axis=1, tiled=True)]
    ppermute x0 -> x16, waiting for transfers between devices: none -> 63.6 us  [shift(): return lax.ppermute(x, axis, [(p, (p + step) % n) for p in range(n)])]
    ppermute x0 -> x16, starting transfers between devices: none -> 20.7 us  [shift(): return lax.ppermute(x, axis, [(p, (p + step) % n) for p in range(n)])]
    all_to_all x1 -> x0, blocking collectives: 19 us -> none  [body(): block = lax.all_to_all(blocks, COL, split_axis=1, concat_axis=2, tiled=True)]
    all_to_all x0 -> x2, starting transfers between devices: none -> 18.4 us  [body(): lax.all_to_all(blocks, COL, split_axis=1, concat_axis=2, tiled=True)]
    dot_general x2 -> x4, matrix products: 17.7 us -> 28.7 us  [the longest x2 14.9 us: body(): jnp.dot(other, ints_rel[1], precision=lax.Precision.HIGH)]
    reduce_scatter x1 -> x2, waiting for transfers between devices: 28.8 us -> 18.8 us  [body(): ladder = lax.psum_scatter(partial, 'row', scatter_dimension=0, tiled=True)]
    all_to_all x0 -> x2, waiting for transfers between devices: none -> 8.68 us  [body(): lax.all_to_all(blocks, COL, split_axis=1, concat_axis=2, tiled=True)]
  transfers between devices with their start and end apart: 3 -> 22, of which waited for: 2 -> 13; matrix products, arithmetic and copies ran while one was open for 7% -> 31% of each run, Pallas kernels for 0% -> 0%
where the time goes in v3:
time: 227 us; the launch traced here: 226 us
  waiting for transfers between devices  91.1 us (40%)
  starting transfers between devices  46.2 us (20%)
  matrix products  29.3 us (13%)
  local copies, waits for them, and re-layouts  26.4 us (12%)
  other arithmetic  19.4 us (9%)
  between operations  13.7 us (6%)
    ppermute x16, waiting for transfers between devices, shift(): return lax.ppermute(x, axis, [(p, (p + step) % n) for p in range(n)])  63.6 us
    ppermute x16, starting transfers between devices, shift(): return lax.ppermute(x, axis, [(p, (p + step) % n) for p in range(n)])  20.7 us
    reduce_scatter x2, waiting for transfers between devices, body(): ladder = lax.psum_scatter(partial, 'row', scatter_dimension=0, tiled=True)  18.8 us
    all_to_all x2, starting transfers between devices, body(): lax.all_to_all(blocks, COL, split_axis=1, concat_axis=2, tiled=True)  18.4 us
    dot_general x2, matrix products, body(): jnp.dot(other, ints_rel[1], precision=lax.Precision.HIGH)  14.9 us
    dot_general x2, matrix products, body(): jnp.dot(own, ints_rel[0], precision=lax.Precision.HIGH)  13.8 us
    unnamed x21, local copies, waits for them, and re-layouts  9.42 us
    all_to_all x2, waiting for transfers between devices, body(): lax.all_to_all(blocks, COL, split_axis=1, concat_axis=2, tiled=True)  8.68 us
  transfers between devices with their start and end apart: 22, of which 13 were waited for; matrix products, arithmetic and copies ran while one was open for 31% of the time, Pallas kernels for 0%

profile of v3, /device:TPU:1, one launch (start us, length us, event | category | flops | bytes accessed | tf_op | source)
XLA Modules:
  0.0 226.1 jit_solution(3976883360371020114)
XLA Ops:
  9.0 3.6 %collective-permute-start = (f32[512,128]{1,0:T(8,128)S(1)}, f32[512,128]{1,0:T(8,128)S(1)}, u32[]{:S(2)}, u32[]{:S(2)}) collective-permute-start(f32[512,128]{1,0:T(8,128)S(1)} %bitcast.43), channel_id=1, source_target_pairs={{0,6},{2,0},{4,2},{6,4},{1,7},{3,1},{5,3},{7,5},{8,14},{10,8},{12,... | collective-permute-start | bytes 786440 | tf_op jit(solution)/shard_map/ppermute | solution.py:14
  12.7 5.0 %collective-permute-done = f32[512,128]{1,0:T(8,128)S(1)} collective-permute-done((f32[512,128]{1,0:T(8,128)S(1)}, f32[512,128]{1,0:T(8,128)S(1)}, u32[]{:S(2)}, u32[]{:S(2)}) %collective-permute-start) | collective-permute-done | bytes 262176 | tf_op jit(solution)/shard_map/ppermute | solution.py:14
  17.7 3.5 %collective-permute-start.1 = (f32[256,128]{1,0:T(8,128)S(1)}, f32[256,128]{1,0:T(8,128)S(1)}, u32[]{:S(2)}, u32[]{:S(2)}) collective-permute-start(f32[256,128]{1,0:T(8,128)S(1)} %slice.55), channel_id=1, source_target_pairs={{0,6},{2,0},{4,2},{6,4},{1,7},{3,1},{5,3},{7,5},{8,14},{10,8},{12,... | collective-permute-start | bytes 393224 | tf_op jit(solution)/shard_map/ppermute | solution.py:14
  21.2 1.8 collective-permute-done.1
  23.1 3.2 %collective-permute-done.3 = f32[256,128]{1,0:T(8,128)S(1)} collective-permute-done((f32[256,128]{1,0:T(8,128)S(1)}, f32[256,128]{1,0:T(8,128)S(1)}, u32[]{:S(2)}, u32[]{:S(2)}) %collective-permute-start.3) | collective-permute-done | bytes 131104 | tf_op jit(solution)/shard_map/ppermute | solution.py:14
  26.3 3.8 %collective-permute-start.4 = (f32[512,512]{1,0:T(8,128)S(1)}, f32[512,512]{1,0:T(8,128)S(1)}, u32[]{:S(2)}, u32[]{:S(2)}) collective-permute-start(f32[512,512]{1,0:T(8,128)S(1)} %pad_maximum_fusion), channel_id=1, source_target_pairs={{0,24},{8,0},{16,8},{24,16},{1,25},{9,1},{17,9},{25,17},{2,26},{10... | collective-permute-start | bytes 3145736 | tf_op jit(solution)/shard_map/ppermute | solution.py:14
  30.2 1.5 collective-permute-start.11
  32.4 3.3 %collective-permute-done.9 = f32[512,128]{1,0:T(8,128)S(1)} collective-permute-done((f32[512,128]{1,0:T(8,128)S(1)}, f32[512,128]{1,0:T(8,128)S(1)}, u32[]{:S(2)}, u32[]{:S(2)}) %collective-permute-start.9) | collective-permute-done | bytes 262176 | tf_op jit(solution)/shard_map/ppermute | solution.py:14
  37.3 12.4 %collective-permute-done.4 = f32[512,512]{1,0:T(8,128)S(1)} collective-permute-done((f32[512,512]{1,0:T(8,128)S(1)}, f32[512,512]{1,0:T(8,128)S(1)}, u32[]{:S(2)}, u32[]{:S(2)}) %collective-permute-start.4) | collective-permute-done | bytes 1048608 | tf_op jit(solution)/shard_map/ppermute | solution.py:14
  49.7 3.5 %collective-permute-start.5 = (f32[256,512]{1,0:T(8,128)S(1)}, f32[256,512]{1,0:T(8,128)S(1)}, u32[]{:S(2)}, u32[]{:S(2)}) collective-permute-start(f32[256,512]{1,0:T(8,128)S(1)} %slice.57), channel_id=1, source_target_pairs={{0,24},{8,0},{16,8},{24,16},{1,25},{9,1},{17,9},{25,17},{2,26},{10... | collective-permute-start | bytes 1572872 | tf_op jit(solution)/shard_map/ppermute | solution.py:14
  57.3 3.4 %collective-permute-done.5 = f32[256,512]{1,0:T(8,128)S(1)} collective-permute-done((f32[256,512]{1,0:T(8,128)S(1)}, f32[256,512]{1,0:T(8,128)S(1)}, u32[]{:S(2)}, u32[]{:S(2)}) %collective-permute-start.5) | collective-permute-done | bytes 524320 | tf_op jit(solution)/shard_map/ppermute | solution.py:14
  60.7 3.2 %collective-permute-done.7 = f32[256,512]{1,0:T(8,128)S(1)} collective-permute-done((f32[256,512]{1,0:T(8,128)S(1)}, f32[256,512]{1,0:T(8,128)S(1)}, u32[]{:S(2)}, u32[]{:S(2)}) %collective-permute-start.7) | collective-permute-done | bytes 524320 | tf_op jit(solution)/shard_map/ppermute | solution.py:14
  66.1 5.0 %collective-permute-start.8 = (f32[512,2048]{1,0:T(8,128)}, f32[512,2048]{1,0:T(8,128)}, u32[]{:S(2)}, u32[]{:S(2)}) collective-permute-start(f32[512,2048]{1,0:T(8,128)} %constant_dynamic-update-slice_fusion), channel_id=1, source_target_pairs={{0,1},{1,0},{2,3},{3,2},{4,5},{5,4},{6,7},{7,6},{8,9},{9,8},{10,11... | collective-permute-start | bytes 12582920 | tf_op jit(solution)/shard_map/ppermute | solution.py:76
  72.1 1.5 collective-permute-start.15
  75.4 21.7 %collective-permute-done.13 = f32[512,512]{1,0:T(8,128)S(1)} collective-permute-done((f32[512,512]{1,0:T(8,128)}, f32[512,512]{1,0:T(8,128)S(1)}, u32[]{:S(2)}, u32[]{:S(2)}) %collective-permute-start.13) | collective-permute-done | bytes 1048608 | tf_op jit(solution)/shard_map/ppermute | solution.py:14
  97.1 1.4 collective-permute-start.14
  102.7 7.1 %collective-permute-done.14 = f32[256,512]{1,0:T(8,128)S(1)} collective-permute-done((f32[256,512]{1,0:T(8,128)S(1)}, f32[256,512]{1,0:T(8,128)S(1)}, u32[]{:S(2)}, u32[]{:S(2)}) %collective-permute-start.14) | collective-permute-done | bytes 524320 | tf_op jit(solution)/shard_map/ppermute | solution.py:14
  109.8 2.5 %collective-permute-done.16 = f32[256,512]{1,0:T(8,128)S(1)} collective-permute-done((f32[256,512]{1,0:T(8,128)S(1)}, f32[256,512]{1,0:T(8,128)S(1)}, u32[]{:S(2)}, u32[]{:S(2)}) %collective-permute-start.16) | collective-permute-done | bytes 524320 | tf_op jit(solution)/shard_map/ppermute | solution.py:14
  114.5 1.9 collective-permute-start.17
  116.5 8.3 %broadcast_multiply_fusion = f32[32,128,512]{2,1,0:T(8,128)} fusion(f32[32,128,512]{2,1,0:T(8,128)} %bitcast.38, f32[32,512]{1,0:T(8,128)S(1)} %bitcast.50), kind=kLoop, calls=%fused_computation.2 | loop fusion | flops 2097152 | bytes 16842752 | tf_op jit(solution)/shard_map/mul | solution.py:62
  124.9 7.7 %gather_fusion = f32[32,128,512]{2,1,0:T(8,128)} fusion(f32[32,128,512]{2,1,0:T(8,128)} %broadcast_multiply_fusion, s32[1024]{0:T(1024)S(1)} %pad_clamp_fusion), kind=kCustom, calls=%fused_computation | custom fusion | bytes 16777344 | tf_op jit(solution)/shard_map/jit(_take)/gather | solution.py:67
  132.6 4.5 %broadcast_select_fusion = f32[32,128,512]{2,1,0:T(8,128)S(1)} fusion(f32[32,128,512]{2,1,0:T(8,128)} %gather_fusion, pred[32]{0:T(512)(128)(4,1)S(1)} %compare_and_fusion), kind=kLoop, calls=%fused_computation.1 | loop fusion | flops 2097152 | bytes 16777248 | tf_op jit(solution)/shard_map/jit(_take)/select_n | solution.py:67
  137.1 1.6 fusion.9
  138.7 7.8 %fusion.11 = f32[512,512]{1,0:T(8,128)S(1)} fusion(f32[512,2048]{1,0:T(8,128)} %collective-permute-done.8, f32[2048,512]{1,0:T(8,128)S(1)} %bitcast.36), kind=kOutput, calls=%fused_computation.55 | convolution fusion | flops 3221225472 | bytes 9437184 | tf_op jit(solution)/shard_map/dot_general | solution.py:77
  146.5 7.0 %convolution_add_fusion.1 = f32[512,512]{1,0:T(8,128)} fusion(f32[512,512]{1,0:T(8,128)S(1)} %fusion.11, f32[512,2048]{1,0:T(8,128)} %constant_dynamic-update-slice_fusion, f32[2048,512]{1,0:T(8,128)S(1)} %bitcast.34), kind=kOutput, calls=%fused_computation.4 | convolution fusion | flops 3221487616 | bytes 10485760 | tf_op jit(solution)/shard_map/dot_general | solution.py:77
  153.9 7.1 %fusion.12 = f32[512,512]{1,0:T(8,128)S(1)} fusion(f32[512,2048]{1,0:T(8,128)} %collective-permute-done.17, f32[2048,512]{1,0:T(8,128)} %bitcast.37), kind=kOutput, calls=%fused_computation.56 | convolution fusion | flops 3221225472 | bytes 9437184 | tf_op jit(solution)/shard_map/dot_general | solution.py:77
  161.0 6.8 %convolution_add_fusion = f32[512,512]{1,0:T(8,128)} fusion(f32[512,512]{1,0:T(8,128)S(1)} %fusion.12, f32[512,2048]{1,0:T(8,128)} %constant_dynamic-update-slice_fusion.6, f32[2048,512]{1,0:T(8,128)S(1)} %bitcast.35), kind=kOutput, calls=%fused_computation.3 | convolution fusion | flops 3221487616 | bytes 10485760 | tf_op jit(solution)/shard_map/dot_general | solution.py:77
  167.8 3.9 %reduce-scatter.3.cloned.1.call-done = f32[128,512]{1,0:T(8,128)} async-done(((f32[512,512]{1,0:T(8,128)}), f32[128,512]{1,0:T(8,128)}) %reduce-scatter.3.cloned.1.call-update) | async-done | bytes 262160 | tf_op jit(solution)/shard_map/reduce_scatter | solution.py:80
  173.5 9.2 %all-to-all-start = ((f32[4,32,4,128]{3,2,0,1:T(4,128)}), f32[4,32,4,128]{3,2,0,1:T(4,128)S(1)}, u32[]{:S(2)}, u32[]{:S(2)}) async-start(f32[4,32,4,128]{3,2,0,1:T(4,128)} %copy.12), calls=%async_computation.1 | async-start | bytes 524288 | tf_op jit(solution)/shard_map/all_to_all | solution.py:82
  182.7 14.9 %reduce-scatter.5.cloned.1.call-done = f32[128,512]{1,0:T(8,128)} async-done(((f32[512,512]{1,0:T(8,128)}), f32[128,512]{1,0:T(8,128)}) %reduce-scatter.5.cloned.1.call-update) | async-done | bytes 262160 | tf_op jit(solution)/shard_map/reduce_scatter | solution.py:80
  199.4 9.2 %all-to-all-start.1 = ((f32[4,32,4,128]{3,2,0,1:T(4,128)}), f32[4,32,4,128]{3,2,0,1:T(4,128)S(1)}, u32[]{:S(2)}, u32[]{:S(2)}) async-start(f32[4,32,4,128]{3,2,0,1:T(4,128)} %copy.14), calls=%async_computation.3 | async-start | bytes 524288 | tf_op jit(solution)/shard_map/all_to_all | solution.py:82
  208.8 8.7 %all-to-all-done.1 = f32[4,32,4,128]{3,2,0,1:T(4,128)S(1)} async-done(((f32[4,32,4,128]{3,2,0,1:T(4,128)}), f32[4,32,4,128]{3,2,0,1:T(4,128)S(1)}, u32[]{:S(2)}, u32[]{:S(2)}) %all-to-all-start.1) | async-done | bytes 262176 | tf_op jit(solution)/shard_map/all_to_all | solution.py:82
  (84 shorter events, 26.6 us)
Async XLA Ops:
  6.5 211.2 %copy-start = (f32[128,128]{1,0:T(8,128)S(1)}, f32[128,128]{1,0:T(8,128)}, u32[]{:S(2)}) copy-start(f32[128,128]{1,0:T(8,128)} %param.7) | copy-start | bytes 196612
  6.5 165.2 %reduce-scatter.3.cloned.1.call-start = ((), (), s32[]{:S(2)}) async-start(), calls=%async_computation.4 | async-start | bytes 1310720 | tf_op jit(solution)/shard_map/reduce_scatter | solution.py:80
  9.0 8.6 %collective-permute-start = (f32[512,128]{1,0:T(8,128)S(1)}, f32[512,128]{1,0:T(8,128)S(1)}, u32[]{:S(2)}, u32[]{:S(2)}) collective-permute-start(f32[512,128]{1,0:T(8,128)S(1)} %bitcast.43), channel_id=1, source_target_pairs={{0,6},{2,0},{4,2},{6,4},{1,7},{3,1},{5,3},{7,5},{8,14},{10,8},{12,... | collective-permute-start | bytes 786440 | tf_op jit(solution)/shard_map/ppermute | solution.py:14
  12.6 8.5 %collective-permute-start.2 = (f32[512,128]{1,0:T(8,128)S(1)}, f32[512,128]{1,0:T(8,128)S(1)}, u32[]{:S(2)}, u32[]{:S(2)}) collective-permute-start(f32[512,128]{1,0:T(8,128)S(1)} %bitcast.44), channel_id=1, source_target_pairs={{0,2},{2,4},{4,6},{6,0},{1,3},{3,5},{5,7},{7,1},{8,10},{10,12},{12... | collective-permute-start | bytes 786440 | tf_op jit(solution)/shard_map/ppermute | solution.py:14
  17.7 5.4 %collective-permute-start.1 = (f32[256,128]{1,0:T(8,128)S(1)}, f32[256,128]{1,0:T(8,128)S(1)}, u32[]{:S(2)}, u32[]{:S(2)}) collective-permute-start(f32[256,128]{1,0:T(8,128)S(1)} %slice.55), channel_id=1, source_target_pairs={{0,6},{2,0},{4,2},{6,4},{1,7},{3,1},{5,3},{7,5},{8,14},{10,8},{12,... | collective-permute-start | bytes 393224 | tf_op jit(solution)/shard_map/ppermute | solution.py:14
  21.1 5.1 %collective-permute-start.3 = (f32[256,128]{1,0:T(8,128)S(1)}, f32[256,128]{1,0:T(8,128)S(1)}, u32[]{:S(2)}, u32[]{:S(2)}) collective-permute-start(f32[256,128]{1,0:T(8,128)S(1)} %slice.56), channel_id=1, source_target_pairs={{0,2},{2,4},{4,6},{6,0},{1,3},{3,5},{5,7},{7,1},{8,10},{10,12},{12... | collective-permute-start | bytes 393224 | tf_op jit(solution)/shard_map/ppermute | solution.py:14
  26.3 23.4 %collective-permute-start.4 = (f32[512,512]{1,0:T(8,128)S(1)}, f32[512,512]{1,0:T(8,128)S(1)}, u32[]{:S(2)}, u32[]{:S(2)}) collective-permute-start(f32[512,512]{1,0:T(8,128)S(1)} %pad_maximum_fusion), channel_id=1, source_target_pairs={{0,24},{8,0},{16,8},{24,16},{1,25},{9,1},{17,9},{25,17},{2,26},{10... | collective-permute-start | bytes 3145736 | tf_op jit(solution)/shard_map/ppermute | solution.py:14
  30.1 23.1 %collective-permute-start.6 = (f32[512,512]{1,0:T(8,128)S(1)}, f32[512,512]{1,0:T(8,128)S(1)}, u32[]{:S(2)}, u32[]{:S(2)}) collective-permute-start(f32[512,512]{1,0:T(8,128)S(1)} %pad_maximum_fusion), channel_id=1, source_target_pairs={{0,8},{8,16},{16,24},{24,0},{1,9},{9,17},{17,25},{25,1},{2,10},{10... | collective-permute-start | bytes 3145736 | tf_op jit(solution)/shard_map/ppermute | solution.py:14
  30.1 5.5 %collective-permute-start.9 = (f32[512,128]{1,0:T(8,128)S(1)}, f32[512,128]{1,0:T(8,128)S(1)}, u32[]{:S(2)}, u32[]{:S(2)}) collective-permute-start(f32[512,128]{1,0:T(8,128)S(1)} %bitcast.39), channel_id=1, source_target_pairs={{0,6},{2,0},{4,2},{6,4},{1,7},{3,1},{5,3},{7,5},{8,14},{10,8},{12,... | collective-permute-start | bytes 786440 | tf_op jit(solution)/shard_map/ppermute | solution.py:14
  30.2 6.5 %collective-permute-start.11 = (f32[512,128]{1,0:T(8,128)S(1)}, f32[512,128]{1,0:T(8,128)S(1)}, u32[]{:S(2)}, u32[]{:S(2)}) collective-permute-start(f32[512,128]{1,0:T(8,128)S(1)} %bitcast.40), channel_id=1, source_target_pairs={{0,2},{2,4},{4,6},{6,0},{1,3},{3,5},{5,7},{7,1},{8,10},{10,12},{12... | collective-permute-start | bytes 786440 | tf_op jit(solution)/shard_map/ppermute | solution.py:14
  35.7 35.4 %collective-permute-start.10 = (f32[256,128]{1,0:T(8,128)S(1)}, f32[256,128]{1,0:T(8,128)S(1)}, u32[]{:S(2)}, u32[]{:S(2)}) collective-permute-start(f32[256,128]{1,0:T(8,128)S(1)} %slice.62), channel_id=1, source_target_pairs={{0,6},{2,0},{4,2},{6,4},{1,7},{3,1},{5,3},{7,5},{8,14},{10,8},{12,... | collective-permute-start | bytes 393224 | tf_op jit(solution)/shard_map/ppermute | solution.py:14
  36.7 34.4 %collective-permute-start.12 = (f32[256,128]{1,0:T(8,128)S(1)}, f32[256,128]{1,0:T(8,128)S(1)}, u32[]{:S(2)}, u32[]{:S(2)}) collective-permute-start(f32[256,128]{1,0:T(8,128)S(1)} %slice.63), channel_id=1, source_target_pairs={{0,2},{2,4},{4,6},{6,0},{1,3},{3,5},{5,7},{7,1},{8,10},{10,12},{12... | collective-permute-start | bytes 393224 | tf_op jit(solution)/shard_map/ppermute | solution.py:14
  49.7 10.9 %collective-permute-start.5 = (f32[256,512]{1,0:T(8,128)S(1)}, f32[256,512]{1,0:T(8,128)S(1)}, u32[]{:S(2)}, u32[]{:S(2)}) collective-permute-start(f32[256,512]{1,0:T(8,128)S(1)} %slice.57), channel_id=1, source_target_pairs={{0,24},{8,0},{16,8},{24,16},{1,25},{9,1},{17,9},{25,17},{2,26},{10... | collective-permute-start | bytes 1572872 | tf_op jit(solution)/shard_map/ppermute | solution.py:14
  53.3 10.7 %collective-permute-start.7 = (f32[256,512]{1,0:T(8,128)S(1)}, f32[256,512]{1,0:T(8,128)S(1)}, u32[]{:S(2)}, u32[]{:S(2)}) collective-permute-start(f32[256,512]{1,0:T(8,128)S(1)} %slice.58), channel_id=1, source_target_pairs={{0,8},{8,16},{16,24},{24,0},{1,9},{9,17},{17,25},{25,1},{2,10},{10... | collective-permute-start | bytes 1572872 | tf_op jit(solution)/shard_map/ppermute | solution.py:14
  66.1 72.6 %collective-permute-start.8 = (f32[512,2048]{1,0:T(8,128)}, f32[512,2048]{1,0:T(8,128)}, u32[]{:S(2)}, u32[]{:S(2)}) collective-permute-start(f32[512,2048]{1,0:T(8,128)} %constant_dynamic-update-slice_fusion), channel_id=1, source_target_pairs={{0,1},{1,0},{2,3},{3,2},{4,5},{5,4},{6,7},{7,6},{8,9},{9,8},{10,11... | collective-permute-start | bytes 12582920 | tf_op jit(solution)/shard_map/ppermute | solution.py:76
  72.1 24.9 %collective-permute-start.13 = (f32[512,512]{1,0:T(8,128)}, f32[512,512]{1,0:T(8,128)S(1)}, u32[]{:S(2)}, u32[]{:S(2)}) collective-permute-start(f32[512,512]{1,0:T(8,128)} %pad_maximum_fusion.1), channel_id=1, source_target_pairs={{0,24},{8,0},{16,8},{24,16},{1,25},{9,1},{17,9},{25,17},{2,26},{10... | collective-permute-start | bytes 3145736 | tf_op jit(solution)/shard_map/ppermute | solution.py:14
  72.1 26.4 %collective-permute-start.15 = (f32[512,512]{1,0:T(8,128)}, f32[512,512]{1,0:T(8,128)S(1)}, u32[]{:S(2)}, u32[]{:S(2)}) collective-permute-start(f32[512,512]{1,0:T(8,128)} %pad_maximum_fusion.1), channel_id=1, source_target_pairs={{0,8},{8,16},{16,24},{24,0},{1,9},{9,17},{17,25},{25,1},{2,10},{10... | collective-permute-start | bytes 3145736 | tf_op jit(solution)/shard_map/ppermute | solution.py:14
  97.1 12.7 %collective-permute-start.14 = (f32[256,512]{1,0:T(8,128)S(1)}, f32[256,512]{1,0:T(8,128)S(1)}, u32[]{:S(2)}, u32[]{:S(2)}) collective-permute-start(f32[256,512]{1,0:T(8,128)S(1)} %slice.64), channel_id=1, source_target_pairs={{0,24},{8,0},{16,8},{24,16},{1,25},{9,1},{17,9},{25,17},{2,26},{10... | collective-permute-start | bytes 1572872 | tf_op jit(solution)/shard_map/ppermute | solution.py:14
  98.5 13.7 %collective-permute-start.16 = (f32[256,512]{1,0:T(8,128)S(1)}, f32[256,512]{1,0:T(8,128)S(1)}, u32[]{:S(2)}, u32[]{:S(2)}) collective-permute-start(f32[256,512]{1,0:T(8,128)S(1)} %slice.65), channel_id=1, source_target_pairs={{0,8},{8,16},{16,24},{24,0},{1,9},{9,17},{17,25},{25,1},{2,10},{10... | collective-permute-start | bytes 1572872 | tf_op jit(solution)/shard_map/ppermute | solution.py:14
  114.5 39.4 %collective-permute-start.17 = (f32[512,2048]{1,0:T(8,128)}, f32[512,2048]{1,0:T(8,128)}, u32[]{:S(2)}, u32[]{:S(2)}) collective-permute-start(f32[512,2048]{1,0:T(8,128)} %constant_dynamic-update-slice_fusion.6), channel_id=1, source_target_pairs={{0,1},{1,0},{2,3},{3,2},{4,5},{5,4},{6,7},{7,6},{8,9},{9,8},{10,11... | collective-permute-start | bytes 12582920 | tf_op jit(solution)/shard_map/ppermute | solution.py:76
  138.7 7.8 %copy-start.3 = (f32[16,128,512]{2,1,0:T(8,128)}, f32[16,128,512]{2,1,0:T(8,128)S(1)}, u32[]{:S(2)}) copy-start(f32[16,128,512]{2,1,0:T(8,128)S(1)} %get-tuple-element.6) | copy-start | bytes 12582916
  138.7 7.8 %copy-start.1 = (f32[16,128,512]{2,1,0:T(8,128)}, f32[16,128,512]{2,1,0:T(8,128)S(1)}, u32[]{:S(2)}) copy-start(f32[16,128,512]{2,1,0:T(8,128)S(1)} %get-tuple-element.5) | copy-start | bytes 12582916
  153.6 44.0 %reduce-scatter.5.cloned.1.call-start = ((), (), s32[]{:S(2)}) async-start(), calls=%async_computation.5 | async-start | bytes 1310720 | tf_op jit(solution)/shard_map/reduce_scatter | solution.py:80
  153.8 7.1 %copy-start.2 = (f32[16,128,512]{2,1,0:T(8,128)S(1)}, f32[16,128,512]{2,1,0:T(8,128)}, u32[]{:S(2)}) copy-start(f32[16,128,512]{2,1,0:T(8,128)} %copy-done.1) | copy-start | bytes 12582916
  173.5 25.9 %all-to-all-start = ((f32[4,32,4,128]{3,2,0,1:T(4,128)}), f32[4,32,4,128]{3,2,0,1:T(4,128)S(1)}, u32[]{:S(2)}, u32[]{:S(2)}) async-start(f32[4,32,4,128]{3,2,0,1:T(4,128)} %copy.12), calls=%async_computation.1 | async-start | bytes 524288 | tf_op jit(solution)/shard_map/all_to_all | solution.py:82
  199.4 18.1 %all-to-all-start.1 = ((f32[4,32,4,128]{3,2,0,1:T(4,128)}), f32[4,32,4,128]{3,2,0,1:T(4,128)S(1)}, u32[]{:S(2)}, u32[]{:S(2)}) async-start(f32[4,32,4,128]{3,2,0,1:T(4,128)} %copy.14), calls=%async_computation.3 | async-start | bytes 524288 | tf_op jit(solution)/shard_map/all_to_all | solution.py:82
Sparse Core Ops, SparseCore 0:
  153.7 17.9 reduce-scatter.2
  174.1 23.4 reduce-scatter.4

commit v4 on v2

--- a/solution.py
+++ b/solution.py
@@ -34,14 +34,16 @@
         integral_mask, (row_id * c_rows, col_id * a_cols), (c_rows, a_cols)
     ).astype(jnp.float32)
     mask_wide = jnp.repeat(mask_local, virt, axis=1)
-    ints = integrals.reshape(n_zy, n_core, k_local, n_local) * mask_wide.reshape(
-        n_zy, n_core, 1, n_local
-    )
+    ints = integrals.reshape(n_zy, n_core, k_local, n_local)
+    masks = mask_wide.reshape(n_zy, n_core, 1, n_local)
+    ints_c0 = ints[:, 0] * masks[:, 0]
+    ints_c1 = ints[:, 1] * masks[:, 1]
 
     own = lax.all_gather(amp_screened, PLANE, axis=1, tiled=True)
     other = lax.ppermute(own, "core", [(0, 1), (1, 0)])
-    ints_own = lax.dynamic_index_in_dim(ints, core_id, 1, keepdims=False)
-    ints_other = lax.dynamic_index_in_dim(ints, 1 - core_id, 1, keepdims=False)
+    first = core_id == 0
+    ints_own = jnp.where(first, ints_c0, ints_c1)
+    ints_other = jnp.where(first, ints_c1, ints_c0)
     own = own.reshape(pairs, n_zy, k_local)
     other = other.reshape(pairs, n_zy, k_local)
     dims = (((1, 2), (0, 1)), ((), ()))
@@ -52,7 +54,14 @@
     ladder = lax.psum_scatter(partial, "row", scatter_dimension=0, tiled=True)
     i_local = pairs // n_row // occ_j
     blocks = ladder.reshape(i_local, occ_j, a_cols, virt)
-    block = lax.all_to_all(blocks, COL, split_axis=1, concat_axis=2, tiled=True)
+    half = i_local // 2
+    block = jnp.concatenate(
+        [
+            lax.all_to_all(blocks[:half], COL, split_axis=1, concat_axis=2, tiled=True),
+            lax.all_to_all(blocks[half:], COL, split_axis=1, concat_axis=2, tiled=True),
+        ],
+        axis=0,
+    )
     return block + jnp.einsum("ac,ijcb->ijab", vv_coupling, block, precision=lax.Precision.HIGHEST)
 
 

time: 168 us -> 177 us (1.054)
  blocking collectives: 19 us -> 0 us
  waiting for transfers between devices: 103 us -> 120 us
  starting transfers between devices: 0.88 us -> 12.4 us
  other arithmetic: 7.3 us -> 2.56 us
  matrix products: 18.7 us -> 22.7 us
    all_to_all x1 -> x0, blocking collectives: 19 us -> none  [body(): block = lax.all_to_all(blocks, COL, split_axis=1, concat_axis=2, tiled=True)]
    all_to_all x0 -> x2, waiting for transfers between devices: none -> 16.7 us  [the longest x1 8.7 us: body(): lax.all_to_all(blocks[half:], COL, split_axis=1, concat_axis=2, tiled=True)]
    all_to_all x0 -> x2, starting transfers between devices: none -> 11.5 us  [the longest x1 7.75 us: body(): lax.all_to_all(blocks[:half], COL, split_axis=1, concat_axis=2, tiled=True)]
    dot_general x1, matrix products: 6.88 us -> 11.9 us  [body(): lax.dot_general(own, ints_own, dims, precision=lax.Precision.HIGH)]
    mul x1 -> x0, other arithmetic: 4.73 us -> none  [body(): integrals.reshape(n_zy, n_core, k_local, n_local)]
    slice x0 -> x6, local copies, waits for them, and re-layouts: none -> 2.79 us  [the longest x3 1.9 us: body(): blocks[:half]]
  transfers between devices with their start and end apart: 3 -> 5, of which waited for: 2 -> 5; matrix products, arithmetic and copies ran while one was open for 7% -> 8% of each run, Pallas kernels for 0% -> 0%
where the time goes in v4:
time: 177 us
  waiting for transfers between devices  120 us (68%)
  matrix products  22.7 us (13%)
  between operations  13.5 us (8%)
  starting transfers between devices  12.4 us (7%)
  local copies, waits for them, and re-layouts  5.7 us (3%)
  other arithmetic  2.56 us (1%)
    all_gather x1, waiting for transfers between devices, body(): own = lax.all_gather(amp_screened, PLANE, axis=1, tiled=True)  74.1 us
    reduce_scatter x1, waiting for transfers between devices, body(): ladder = lax.psum_scatter(partial, 'row', scatter_dimension=0, tiled=True)  29 us
    dot_general x1, matrix products, body(): lax.dot_general(own, ints_own, dims, precision=lax.Precision.HIGH)  11.9 us
    dot_general x1, matrix products, body(): lax.dot_general(other, ints_other, dims, precision=lax.Precision.HIGH)  10.2 us
    all_to_all x1, waiting for transfers between devices, body(): lax.all_to_all(blocks[half:], COL, split_axis=1, concat_axis=2, tiled=True)  8.7 us
    all_to_all x1, waiting for transfers between devices, body(): lax.all_to_all(blocks[:half], COL, split_axis=1, concat_axis=2, tiled=True)  8.02 us
    all_to_all x1, starting transfers between devices, body(): lax.all_to_all(blocks[:half], COL, split_axis=1, concat_axis=2, tiled=True)  7.75 us
    all_to_all x1, starting transfers between devices, body(): lax.all_to_all(blocks[half:], COL, split_axis=1, concat_axis=2, tiled=True)  3.76 us
  transfers between devices with their start and end apart: 5, of which 5 were waited for; matrix products, arithmetic and copies ran while one was open for 8% of the time, Pallas kernels for 0%

profile of v4, /device:TPU:1, one launch (start us, length us, event | category | flops | bytes accessed | tf_op | source)
XLA Modules:
  0.0 177.0 jit_solution(2311168115739842493)
XLA Ops:
  6.5 0.9 convert_reduce_fusion
  7.5 0.1 mul.56
  7.5 0.1 mul.57
  7.6 1.2 copy.19
  8.9 0.8 broadcast_multiply_fusion
  9.7 0.0 all-gather.2.cloned.1.call-update
  9.7 0.0 reduce-scatter.2.cloned.1.call-start
  9.8 74.1 %all-gather.2.cloned.1.call-done = f32[1024,2048]{0,1:T(8,128)} async-done(((f32[1024,128]{0,1:T(8,128)}), f32[1024,2048]{0,1:T(8,128)}) %all-gather.2.cloned.1.call-update) | async-done | bytes 8388624 | tf_op jit(solution)/shard_map/all_gather | solution.py:42
  83.9 0.8 collective-permute-start
  84.7 0.8 dynamic-slice_convert_fusion
  85.5 0.1 broadcast_in_dim.4
  85.6 0.1 reshape_reshape.3
  85.7 0.1 fusion.25
  85.7 0.0 slice-start.1
  85.8 11.9 %fusion.4 = f32[1024,512,1]{1,0,2:T(8,128)S(1)} fusion(f32[1024,16,128]{0,2,1:T(8,128)} %bitcast.65, f32[16,2,128,512]{3,2,1,0:T(8,128)} %bitcast.61, f32[16,512]{1,0:T(8,128)S(1)} %get-tuple-element.9, f32[16,512]{1,0:T(8,128)S(1)} %get-tuple-element.10, pred[]{:T(512)S(6)} %eq.3), kind=kOutput, calls=%fused_computation.6 | convolution fusion | flops 6445596672 | bytes 18939904 | tf_op jit(solution)/shard_map/dot_general | solution.py:50
  97.7 0.1 collective-permute-done
  97.8 10.2 %bitcast_add_fusion = f32[1024,512]{1,0:T(8,128)} fusion(f32[1024,512,1]{1,0,2:T(8,128)S(1)} %fusion.4, f32[1024,16,128]{0,2,1:T(8,128)} %bitcast.4, f32[16,2,128,512]{3,2,1,0:T(8,128)S(1)} %bitcast.64, f32[16,512]{1,0:T(8,128)S(1)} %get-tuple-element.9, f32[16,512]{1,0:T(8,128)S(1)} %get-tuple-element.10, pred[]{:T(512)S(6)} %eq.3), kind=kOutput, calls=%fused_computation.10 | convolution fusion | flops 6446120960 | bytes 21037056 | tf_op jit(solution)/shard_map/dot_general | solution.py:50
  108.1 0.0 reduce-scatter.2.cloned.1.call-update
  108.1 29.0 %reduce-scatter.2.cloned.1.call-done = f32[256,512]{1,0:T(8,128)} async-done(((f32[1024,512]{1,0:T(8,128)}), f32[256,512]{1,0:T(8,128)}) %reduce-scatter.2.cloned.1.call-update) | async-done | bytes 524304 | tf_op jit(solution)/shard_map/reduce_scatter | solution.py:54
  137.1 1.1 fusion.24
  138.2 0.1 slice.29
  138.3 0.7 copy.24
  139.0 7.8 %all-to-all-start = ((f32[4,32,4,128]{3,2,0,1:T(4,128)}), f32[4,32,4,128]{3,2,0,1:T(4,128)S(1)}, u32[]{:S(2)}, u32[]{:S(2)}) async-start(f32[4,32,4,128]{3,2,0,1:T(4,128)} %copy.24), calls=%async_computation.1 | async-start | bytes 524288 | tf_op jit(solution)/shard_map/all_to_all | solution.py:60
  146.8 0.1 slice.31
  146.9 0.7 copy.26
  147.7 8.0 %all-to-all-done = f32[4,32,4,128]{3,2,0,1:T(4,128)S(1)} async-done(((f32[4,32,4,128]{3,2,0,1:T(4,128)}), f32[4,32,4,128]{3,2,0,1:T(4,128)S(1)}, u32[]{:S(2)}, u32[]{:S(2)}) %all-to-all-start) | async-done | bytes 262176 | tf_op jit(solution)/shard_map/all_to_all | solution.py:60
  155.7 3.8 %all-to-all-start.1 = ((f32[4,32,4,128]{3,2,0,1:T(4,128)}), f32[4,32,4,128]{3,2,0,1:T(4,128)S(1)}, u32[]{:S(2)}, u32[]{:S(2)}) async-start(f32[4,32,4,128]{3,2,0,1:T(4,128)} %copy.26), calls=%async_computation.2 | async-start | bytes 524288 | tf_op jit(solution)/shard_map/all_to_all | solution.py:61
  159.5 0.1 copy.28
  159.6 8.7 %all-to-all-done.1 = f32[4,32,4,128]{3,2,0,1:T(4,128)S(1)} async-done(((f32[4,32,4,128]{3,2,0,1:T(4,128)}), f32[4,32,4,128]{3,2,0,1:T(4,128)S(1)}, u32[]{:S(2)}, u32[]{:S(2)}) %all-to-all-start.1) | async-done | bytes 262176 | tf_op jit(solution)/shard_map/all_to_all | solution.py:61
  168.4 0.1 copy.29
  168.5 0.6 fusion.20
  169.1 1.0 copy.30
  (10 shorter events, 0.1 us)
Async XLA Ops:
  6.5 162.0 %copy-start = (f32[128,128]{1,0:T(8,128)S(1)}, f32[128,128]{1,0:T(8,128)}, u32[]{:S(2)}) copy-start(f32[128,128]{1,0:T(8,128)} %param.7) | copy-start | bytes 196612
  6.5 77.3 %all-gather.2.cloned.1.call-start = ((), (), s32[]{:S(2)}) async-start(), calls=%async_computation.3 | async-start | bytes 8912896 | tf_op jit(solution)/shard_map/all_gather | solution.py:42
  9.7 127.4 %reduce-scatter.2.cloned.1.call-start = ((), (), s32[]{:S(2)}) async-start(), calls=%async_computation.4 | async-start | bytes 2621440 | tf_op jit(solution)/shard_map/reduce_scatter | solution.py:54
  83.9 14.0 %collective-permute-start = (f32[1024,2048]{0,1:T(8,128)}, f32[1024,2048]{0,1:T(8,128)}, u32[]{:S(2)}, u32[]{:S(2)}) collective-permute-start(f32[1024,2048]{0,1:T(8,128)} %all-gather.2.cloned.1.call-done), channel_id=1, source_target_pairs={{0,1},{1,0},{2,3},{3,2},{4,5},{5,4},{6,7},{7,6},{8,9},{9,8},{10,11... | collective-permute-start | bytes 25165832 | tf_op jit(solution)/shard_map/ppermute | solution.py:43
  85.7 12.2 %slice-start = ((s8[8388608]{0:T(1024)(128)(4,1)}), s8[4194304]{0:T(1024)(128)(4,1)S(1)}, s32[]{:S(2)}) async-start(s8[8388608]{0:T(1024)(128)(4,1)} %bitcast.62), calls=%async_computation.5 | async-start | bytes 8388608
  85.7 12.1 %slice-start.1 = ((s8[8388608]{0:T(1024)(128)(4,1)}), s8[4194304]{0:T(1024)(128)(4,1)S(1)}, s32[]{:S(2)}) async-start(s8[8388608]{0:T(1024)(128)(4,1)} %bitcast.62), calls=%async_computation.6 | async-start | bytes 8388608
  139.0 16.6 %all-to-all-start = ((f32[4,32,4,128]{3,2,0,1:T(4,128)}), f32[4,32,4,128]{3,2,0,1:T(4,128)S(1)}, u32[]{:S(2)}, u32[]{:S(2)}) async-start(f32[4,32,4,128]{3,2,0,1:T(4,128)} %copy.24), calls=%async_computation.1 | async-start | bytes 524288 | tf_op jit(solution)/shard_map/all_to_all | solution.py:60
  155.7 12.7 %all-to-all-start.1 = ((f32[4,32,4,128]{3,2,0,1:T(4,128)}), f32[4,32,4,128]{3,2,0,1:T(4,128)S(1)}, u32[]{:S(2)}, u32[]{:S(2)}) async-start(f32[4,32,4,128]{3,2,0,1:T(4,128)} %copy.26), calls=%async_computation.2 | async-start | bytes 524288 | tf_op jit(solution)/shard_map/all_to_all | solution.py:61
Sparse Core Ops, SparseCore 0:
  9.9 73.9 all-gather.1
  108.2 28.8 reduce-scatter.1

commit v5 on v4

--- a/solution.py
+++ b/solution.py
@@ -51,17 +51,13 @@
         other, ints_other, dims, precision=lax.Precision.HIGH
     )
 
-    ladder = lax.psum_scatter(partial, "row", scatter_dimension=0, tiled=True)
+    pieces = lax.all_to_all(
+        partial.reshape(n_row, pairs // n_row, n_local), "row", split_axis=0, concat_axis=0, tiled=True
+    )
+    ladder = pieces.sum(axis=0)
     i_local = pairs // n_row // occ_j
     blocks = ladder.reshape(i_local, occ_j, a_cols, virt)
-    half = i_local // 2
-    block = jnp.concatenate(
-        [
-            lax.all_to_all(blocks[:half], COL, split_axis=1, concat_axis=2, tiled=True),
-            lax.all_to_all(blocks[half:], COL, split_axis=1, concat_axis=2, tiled=True),
-        ],
-        axis=0,
-    )
+    block = lax.all_to_all(blocks, COL, split_axis=1, concat_axis=2, tiled=True)
     return block + jnp.einsum("ac,ijcb->ijab", vv_coupling, block, precision=lax.Precision.HIGHEST)
 
 

time: 177 us -> 165 us (0.932)
  blocking collectives: 0 us -> 47.6 us
  waiting for transfers between devices: 120 us -> 74.3 us
  starting transfers between devices: 12.4 us -> 0.84 us
  local copies, waits for them, and re-layouts: 5.7 us -> 3.19 us
    all_to_all x0 -> x2, blocking collectives: none -> 47.6 us  [the longest x1 29.2 us: body(): lax.all_to_all(partial.reshape(n_row, pairs // n_row, n_local), 'row', sp...]
    reduce_scatter x1 -> x0, waiting for transfers between devices: 29 us -> none  [body(): ladder = lax.psum_scatter(partial, 'row', scatter_dimension=0, tiled=True)]
    all_to_all x2 -> x0, waiting for transfers between devices: 16.7 us -> none  [the longest x1 8.7 us: body(): lax.all_to_all(blocks[half:], COL, split_axis=1, concat_axis=2, tiled=True)]
    all_to_all x2 -> x0, starting transfers between devices: 11.5 us -> none  [the longest x1 7.75 us: body(): lax.all_to_all(blocks[:half], COL, split_axis=1, concat_axis=2, tiled=True)]
    slice x5 -> x0, local copies, waits for them, and re-layouts: 2.74 us -> none  [the longest x3 1.9 us: body(): blocks[:half]]
  transfers between devices with their start and end apart: 5 -> 2, of which waited for: 5 -> 2; matrix products, arithmetic and copies ran while one was open for 8% -> 8% of each run, Pallas kernels for 0% -> 0%
where the time goes in v5:
time: 165 us; the launch traced here: 164 us
  waiting for transfers between devices  74.3 us (45%)
  blocking collectives  47.6 us (29%)
  matrix products  22.2 us (13%)
  between operations  13.5 us (8%)
  local copies, waits for them, and re-layouts  3.19 us (2%)
  other arithmetic  2.81 us (2%)
    all_gather x1, waiting for transfers between devices, body(): own = lax.all_gather(amp_screened, PLANE, axis=1, tiled=True)  74.1 us
    all_to_all x1, blocking collectives, body(): lax.all_to_all(partial.reshape(n_row, pairs // n_row, n_local), 'row', sp...  29.2 us
    all_to_all x1, blocking collectives, body(): block = lax.all_to_all(blocks, COL, split_axis=1, concat_axis=2, tiled=True)  18.4 us
    dot_general x1, matrix products, body(): lax.dot_general(own, ints_own, dims, precision=lax.Precision.HIGH)  11.9 us
    dot_general x1, matrix products, body(): lax.dot_general(other, ints_other, dims, precision=lax.Precision.HIGH)  9.29 us
  transfers between devices with their start and end apart: 2, of which 2 were waited for; matrix products, arithmetic and copies ran while one was open for 8% of the time, Pallas kernels for 0%

profile of v5, /device:TPU:1, one launch (start us, length us, event | category | flops | bytes accessed | tf_op | source)
XLA Modules:
  0.0 164.5 jit_solution(8563197067422699054)
XLA Ops:
  6.5 0.0 copy-start
  6.5 0.0 all-gather.2.cloned.1.call-start
  6.5 0.9 convert_reduce_fusion
  7.5 0.1 mul.56
  7.5 0.1 mul.57
  7.6 1.2 copy.19
  8.9 0.8 broadcast_multiply_fusion
  9.7 0.0 all-gather.2.cloned.1.call-update
  9.7 74.1 %all-gather.2.cloned.1.call-done = f32[1024,2048]{0,1:T(8,128)} async-done(((f32[1024,128]{0,1:T(8,128)}), f32[1024,2048]{0,1:T(8,128)}) %all-gather.2.cloned.1.call-update) | async-done | bytes 8388624 | tf_op jit(solution)/shard_map/all_gather | solution.py:42
  83.9 0.8 collective-permute-start
  84.7 0.8 dynamic-slice_convert_fusion
  85.5 0.1 broadcast_in_dim.4
  85.6 0.1 reshape_reshape.3
  85.7 0.0 slice-start
  85.7 0.1 fusion.23
  85.7 0.0 slice-start.1
  85.8 11.9 %fusion.4 = f32[1024,512,1]{1,0,2:T(8,128)S(1)} fusion(f32[1024,16,128]{0,2,1:T(8,128)} %bitcast.64, f32[16,2,128,512]{3,2,1,0:T(8,128)} %bitcast.60, f32[16,512]{1,0:T(8,128)S(1)} %get-tuple-element.7, f32[16,512]{1,0:T(8,128)S(1)} %get-tuple-element.8, pred[]{:T(512)S(6)} %eq.3), kind=kOutput, calls=%fused_computation.6 | convolution fusion | flops 6445596672 | bytes 18939904 | tf_op jit(solution)/shard_map/dot_general | solution.py:50
  97.7 0.1 collective-permute-done
  97.8 0.0 slice-done
  97.8 0.0 slice-done.1
  97.8 9.3 %bitcast_add_fusion = f32[1024,512]{1,0:T(8,128)S(1)} fusion(f32[1024,512,1]{1,0,2:T(8,128)S(1)} %fusion.4, f32[1024,16,128]{0,2,1:T(8,128)} %bitcast.4, f32[16,2,128,512]{3,2,1,0:T(8,128)S(1)} %bitcast.63, f32[16,512]{1,0:T(8,128)S(1)} %get-tuple-element.7, f32[16,512]{1,0:T(8,128)S(1)} %get-tuple-element.8, pred[]{:T(512)S(6)} %eq.3), kind=kOutput, calls=%fused_computation.10 | convolution fusion | flops 6446120960 | bytes 21037056 | tf_op jit(solution)/shard_map/dot_general | solution.py:50
  107.1 29.2 %all_to_all.17 = f32[4,256,512]{2,1,0:T(8,128)S(1)} all-to-all(f32[4,256,512]{2,1,0:T(8,128)S(1)} %bitcast.59), channel_id=1, replica_groups=mesh['row'=4,'z'=4,'y'=4,'core'=2] {'row'}, dimensions={0} | all-to-all | bytes 4194304 | tf_op jit(solution)/shard_map/all_to_all | solution.py:54
  136.4 0.2 reduce_sum.9
  136.6 0.2 reshape.35
  136.8 0.1 copy.24
  137.0 18.4 %all_to_all.18 = f32[8,32,4,128]{3,2,0,1:T(4,128)S(1)} all-to-all(f32[8,32,4,128]{3,2,0,1:T(4,128)S(1)} %copy.24), channel_id=1, replica_groups=mesh['row'=4,'z'=4,'y'=4,'core'=2] {'z','y','core'}, dimensions={1} | all-to-all | bytes 1048576 | tf_op jit(solution)/shard_map/all_to_all | solution.py:60
  155.4 0.2 copy.28
  155.6 0.0 copy-done
  155.6 1.0 fusion.20
  156.6 1.0 copy.29
  (3 shorter events, 0.0 us)
Async XLA Ops:
  6.5 149.1 %copy-start = (f32[128,128]{1,0:T(8,128)S(1)}, f32[128,128]{1,0:T(8,128)}, u32[]{:S(2)}) copy-start(f32[128,128]{1,0:T(8,128)} %param.7) | copy-start | bytes 196612
  6.5 77.3 %all-gather.2.cloned.1.call-start = ((), (), s32[]{:S(2)}) async-start(), calls=%async_computation.2 | async-start | bytes 8912896 | tf_op jit(solution)/shard_map/all_gather | solution.py:42
  83.9 14.0 %collective-permute-start = (f32[1024,2048]{0,1:T(8,128)}, f32[1024,2048]{0,1:T(8,128)}, u32[]{:S(2)}, u32[]{:S(2)}) collective-permute-start(f32[1024,2048]{0,1:T(8,128)} %all-gather.2.cloned.1.call-done), channel_id=1, source_target_pairs={{0,1},{1,0},{2,3},{3,2},{4,5},{5,4},{6,7},{7,6},{8,9},{9,8},{10,11... | collective-permute-start | bytes 25165832 | tf_op jit(solution)/shard_map/ppermute | solution.py:43
  85.7 12.2 %slice-start = ((s8[8388608]{0:T(1024)(128)(4,1)}), s8[4194304]{0:T(1024)(128)(4,1)S(1)}, s32[]{:S(2)}) async-start(s8[8388608]{0:T(1024)(128)(4,1)} %bitcast.61), calls=%async_computation.3 | async-start | bytes 8388608
  85.7 12.1 %slice-start.1 = ((s8[8388608]{0:T(1024)(128)(4,1)}), s8[4194304]{0:T(1024)(128)(4,1)S(1)}, s32[]{:S(2)}) async-start(s8[8388608]{0:T(1024)(128)(4,1)} %bitcast.61), calls=%async_computation.4 | async-start | bytes 8388608
Sparse Core Ops, SparseCore 0:
  9.9 73.9 all-gather.1

commit v6 on v5

--- a/solution.py
+++ b/solution.py
@@ -21,11 +21,8 @@
     occ_i = amp_mask.shape[0]
     occ_j = pairs // occ_i
 
-    c_own = row_id * n_col + col_id
-    amp_col = lax.dynamic_slice_in_dim(amp_mask, c_own, 1, axis=1).astype(jnp.float32)
-    amp_screened = (amplitudes.reshape(occ_i, occ_j, k_local) * amp_col[:, :, None]).reshape(
-        pairs, k_local
-    )
+    amp_row = lax.dynamic_slice_in_dim(amp_mask, row_id * n_col, n_col, axis=1).astype(jnp.float32)
+    amp_row = amp_row.reshape(occ_i, n_zy, n_core)
 
     c_rows = virt // n_row
     a_cols = virt // n_col
@@ -39,13 +36,19 @@
     ints_c0 = ints[:, 0] * masks[:, 0]
     ints_c1 = ints[:, 1] * masks[:, 1]
 
-    own = lax.all_gather(amp_screened, PLANE, axis=1, tiled=True)
+    own = lax.all_gather(amplitudes, PLANE, axis=1, tiled=True)
     other = lax.ppermute(own, "core", [(0, 1), (1, 0)])
     first = core_id == 0
     ints_own = jnp.where(first, ints_c0, ints_c1)
     ints_other = jnp.where(first, ints_c1, ints_c0)
-    own = own.reshape(pairs, n_zy, k_local)
-    other = other.reshape(pairs, n_zy, k_local)
+    amp_own = jnp.where(first, amp_row[:, :, 0], amp_row[:, :, 1])
+    amp_other = jnp.where(first, amp_row[:, :, 1], amp_row[:, :, 0])
+    own = (own.reshape(occ_i, occ_j, n_zy, k_local) * amp_own[:, None, :, None]).reshape(
+        pairs, n_zy, k_local
+    )
+    other = (other.reshape(occ_i, occ_j, n_zy, k_local) * amp_other[:, None, :, None]).reshape(
+        pairs, n_zy, k_local
+    )
     dims = (((1, 2), (0, 1)), ((), ()))
     partial = lax.dot_general(own, ints_own, dims, precision=lax.Precision.HIGH) + lax.dot_general(
         other, ints_other, dims, precision=lax.Precision.HIGH

time: 165 us -> 184 us (1.12)
  waiting for transfers between devices: 74.3 us -> 82.2 us
  matrix products: 22.2 us -> 29.6 us
  local copies, waits for them, and re-layouts: 3.19 us -> 8.44 us
    all_gather x1, waiting for transfers between devices: 74.1 us -> 81.4 us  [body(): own = lax.all_gather(amplitudes, PLANE, axis=1, tiled=True)]
    mul x2 -> x4, local copies, waits for them, and re-layouts: 0.15 us -> 4.69 us  [the longest x2 2.35 us: body(): own.reshape(occ_i, occ_j, n_zy, k_local) * amp_own[:, None, :, None]]
    dot_general x1, matrix products: 9.29 us -> 13.3 us  [body(): lax.dot_general(other, ints_other, dims, precision=lax.Precision.HIGH)]
    dot_general x1, matrix products: 11.9 us -> 15.3 us  [body(): lax.dot_general(own, ints_own, dims, precision=lax.Precision.HIGH)]
  transfers between devices with their start and end apart: 2 -> 2, of which waited for: 2 -> 1; matrix products, arithmetic and copies ran while one was open for 8% -> 11% of each run, Pallas kernels for 0% -> 0%
where the time goes in v6:
time: 184 us
  waiting for transfers between devices  82.2 us (45%)
  blocking collectives  47.3 us (26%)
  matrix products  29.6 us (16%)
  between operations  13.5 us (7%)
  local copies, waits for them, and re-layouts  8.44 us (5%)
  starting transfers between devices  2.04 us (1%)
    all_gather x1, waiting for transfers between devices, body(): own = lax.all_gather(amplitudes, PLANE, axis=1, tiled=True)  81.4 us
    all_to_all x1, blocking collectives, body(): lax.all_to_all(partial.reshape(n_row, pairs // n_row, n_local), 'row', sp...  29.9 us
    all_to_all x1, blocking collectives, body(): block = lax.all_to_all(blocks, COL, split_axis=1, concat_axis=2, tiled=True)  17.4 us
    dot_general x1, matrix products, body(): lax.dot_general(own, ints_own, dims, precision=lax.Precision.HIGH)  15.3 us
    dot_general x1, matrix products, body(): lax.dot_general(other, ints_other, dims, precision=lax.Precision.HIGH)  13.3 us
  transfers between devices with their start and end apart: 2, of which 1 were waited for; matrix products, arithmetic and copies ran while one was open for 11% of the time, Pallas kernels for 0%

profile of v6, /device:TPU:1, one launch (start us, length us, event | category | flops | bytes accessed | tf_op | source)
XLA Modules:
  0.0 184.1 jit_solution(10301706780686218349)
XLA Ops:
  6.5 0.0 copy-start
  6.5 0.0 all-gather.2.cloned.1.call-start
  6.5 0.7 all-gather.2.cloned.1.call-update
  7.3 81.4 %all-gather.2.cloned.1.call-done = f32[1024,2048]{1,0:T(8,128)} async-done(((f32[1024,128]{1,0:T(8,128)}), f32[1024,2048]{1,0:T(8,128)}) %all-gather.2.cloned.1.call-update) | async-done | bytes 8388624 | tf_op jit(solution)/shard_map/all_gather | solution.py:39
  88.7 2.0 %collective-permute-start = (f32[1024,2048]{1,0:T(8,128)}, f32[1024,2048]{1,0:T(8,128)}, u32[]{:S(2)}, u32[]{:S(2)}) collective-permute-start(f32[1024,2048]{1,0:T(8,128)} %all-gather.2.cloned.1.call-done), channel_id=1, source_target_pairs={{0,1},{1,0},{2,3},{3,2},{4,5},{5,4},{6,7},{7,6},{8,9},{9,8},{10,11... | collective-permute-start | bytes 25165832 | tf_op jit(solution)/shard_map/ppermute | solution.py:40
  90.7 0.8 dynamic-slice_convert_fusion
  91.5 0.1 broadcast_in_dim.2
  91.6 0.1 reshape_reshape.3
  91.7 0.8 constant_dynamic-slice_fusion
  92.5 0.1 copy.38
  92.6 0.1 copy.24
  92.7 0.1 copy.28
  92.7 0.0 copy-start.1
  92.7 0.1 fusion.31
  92.9 2.3 %mul.76 = f32[1024,16,128]{2,1,0:T(8,128)S(1)} broadcast(f32[1024,16]{1,0:T(8,128)S(1)} %bitcast.95), dimensions={0,1} | broadcast | bytes 8454144 | tf_op jit(solution)/shard_map/mul | solution.py:46
  95.2 0.9 copy-done.1
  96.1 15.3 %fusion.5 = f32[1024,512,1]{1,0,2:T(8,128)S(1)} fusion(f32[16,2,128,512]{3,2,1,0:T(8,128)} %bitcast.91, f32[16,512]{1,0:T(8,128)S(1)} %get-tuple-element.9, f32[16,512]{1,0:T(8,128)S(1)} %get-tuple-element.10, pred[]{:T(512)S(6)} %eq.3, f32[1024,2048]{1,0:T(8,128)S(1)} %copy-done.1, f32[128,8,16,128]{3,2,1,0:T(8,128)S(1)} %bitcast.89), kind=kOutput, calls=%fused_computation.7 | convolution fusion | flops 6447693824 | bytes 27328512 | tf_op jit(solution)/shard_map/dot_general | solution.py:53
  111.5 0.0 collective-permute-done
  111.5 2.3 %mul.91 = f32[1024,16,128]{2,1,0:T(8,128)S(1)} broadcast(f32[1024,16]{1,0:T(8,128)S(1)} %bitcast.96), dimensions={0,1} | broadcast | bytes 8454144 | tf_op jit(solution)/shard_map/mul | solution.py:49
  113.9 13.3 %bitcast_add_fusion = f32[1024,512]{1,0:T(8,128)S(1)} fusion(f32[1024,512,1]{1,0,2:T(8,128)S(1)} %fusion.5, f32[16,2,128,512]{3,2,1,0:T(8,128)} %bitcast.92, f32[16,512]{1,0:T(8,128)S(1)} %get-tuple-element.9, f32[16,512]{1,0:T(8,128)S(1)} %get-tuple-element.10, pred[]{:T(512)S(6)} %eq.3, f32[1024,2048]{1,0:T(8,128)} %collective-permute-done, ...), kind=kOutput, calls=%fused_computation.18 | convolution fusion | flops 6448218112 | bytes 29425664 | tf_op jit(solution)/shard_map/dot_general | solution.py:53
  127.1 29.9 %all_to_all.17 = f32[4,256,512]{2,1,0:T(8,128)S(1)} all-to-all(f32[4,256,512]{2,1,0:T(8,128)S(1)} %bitcast.90), channel_id=1, replica_groups=mesh['row'=4,'z'=4,'y'=4,'core'=2] {'row'}, dimensions={0} | all-to-all | bytes 4194304 | tf_op jit(solution)/shard_map/all_to_all | solution.py:57
  157.0 0.2 reduce_sum.9
  157.3 0.2 reshape.61
  157.5 0.1 copy.30
  157.6 17.4 %all_to_all.18 = f32[8,32,4,128]{3,2,0,1:T(4,128)S(1)} all-to-all(f32[8,32,4,128]{3,2,0,1:T(4,128)S(1)} %copy.30), channel_id=1, replica_groups=mesh['row'=4,'z'=4,'y'=4,'core'=2] {'z','y','core'}, dimensions={1} | all-to-all | bytes 1048576 | tf_op jit(solution)/shard_map/all_to_all | solution.py:63
  175.0 0.2 copy.34
  175.3 0.0 copy-done
  175.3 1.0 fusion.28
  176.3 1.0 copy.35
  (6 shorter events, 0.1 us)
Async XLA Ops:
  6.5 168.7 %copy-start = (f32[128,128]{1,0:T(8,128)S(1)}, f32[128,128]{1,0:T(8,128)}, u32[]{:S(2)}) copy-start(f32[128,128]{1,0:T(8,128)} %param.7) | copy-start | bytes 196612
  6.5 82.2 %all-gather.2.cloned.1.call-start = ((), (), s32[]{:S(2)}) async-start(), calls=%async_computation.2 | async-start | bytes 8912896 | tf_op jit(solution)/shard_map/all_gather | solution.py:39
  88.7 22.8 %collective-permute-start = (f32[1024,2048]{1,0:T(8,128)}, f32[1024,2048]{1,0:T(8,128)}, u32[]{:S(2)}, u32[]{:S(2)}) collective-permute-start(f32[1024,2048]{1,0:T(8,128)} %all-gather.2.cloned.1.call-done), channel_id=1, source_target_pairs={{0,1},{1,0},{2,3},{3,2},{4,5},{5,4},{6,7},{7,6},{8,9},{9,8},{10,11... | collective-permute-start | bytes 25165832 | tf_op jit(solution)/shard_map/ppermute | solution.py:40
  92.7 3.4 %copy-start.1 = (f32[1024,2048]{1,0:T(8,128)S(1)}, f32[1024,2048]{1,0:T(8,128)}, u32[]{:S(2)}) copy-start(f32[1024,2048]{1,0:T(8,128)} %all-gather.2.cloned.1.call-done) | copy-start | bytes 25165828
Sparse Core Ops, SparseCore 0:
  9.4 79.2 all-gather.1

commit v7 on v5

--- a/solution.py
+++ b/solution.py
@@ -51,13 +51,12 @@
         other, ints_other, dims, precision=lax.Precision.HIGH
     )
 
-    pieces = lax.all_to_all(
-        partial.reshape(n_row, pairs // n_row, n_local), "row", split_axis=0, concat_axis=0, tiled=True
-    )
-    ladder = pieces.sum(axis=0)
     i_local = pairs // n_row // occ_j
-    blocks = ladder.reshape(i_local, occ_j, a_cols, virt)
-    block = lax.all_to_all(blocks, COL, split_axis=1, concat_axis=2, tiled=True)
+    buf = partial.reshape(n_row, i_local, occ_j, a_cols, virt).transpose(0, 2, 1, 3, 4)
+    buf = buf.reshape(n_row * occ_j, i_local, a_cols, virt)
+    recv = lax.all_to_all(buf, ("row",) + COL, split_axis=0, concat_axis=0, tiled=True)
+    summed = recv.reshape(n_row, n_col, i_local, a_cols, virt).sum(axis=0)
+    block = summed.transpose(1, 0, 2, 3).reshape(i_local, 1, n_col * a_cols, virt)
     return block + jnp.einsum("ac,ijcb->ijab", vv_coupling, block, precision=lax.Precision.HIGHEST)
 
 

time: 165 us -> 158 us (0.958)
  blocking collectives: 47.6 us -> 37.6 us
  local copies, waits for them, and re-layouts: 3.19 us -> 5.99 us
    all_to_all x2 -> x1, blocking collectives: 47.6 us -> 37.6 us  [body(): lax.all_to_all(buf, ('row',) + COL, split_axis=0, concat_axis=0, tiled=True)]
    reshape x2 -> x3, local copies, waits for them, and re-layouts: 0.32 us -> 3.37 us  [the longest x2 3.15 us: body(): partial.reshape(n_row, i_local, occ_j, a_cols, virt)]
where the time goes in v7:
time: 158 us
  waiting for transfers between devices  74.3 us (47%)
  blocking collectives  37.6 us (24%)
  matrix products  23.2 us (15%)
  between operations  13.5 us (9%)
  local copies, waits for them, and re-layouts  5.99 us (4%)
  other arithmetic  2.81 us (2%)
    all_gather x1, waiting for transfers between devices, body(): own = lax.all_gather(amp_screened, PLANE, axis=1, tiled=True)  74.1 us
    all_to_all x1, blocking collectives, body(): lax.all_to_all(buf, ('row',) + COL, split_axis=0, concat_axis=0, tiled=True)  37.6 us
    dot_general x1, matrix products, body(): lax.dot_general(own, ints_own, dims, precision=lax.Precision.HIGH)  11.9 us
    dot_general x1, matrix products, body(): lax.dot_general(other, ints_other, dims, precision=lax.Precision.HIGH)  10.2 us
  transfers between devices with their start and end apart: 2, of which 2 were waited for; matrix products, arithmetic and copies ran while one was open for 8% of the time, Pallas kernels for 0%

profile of v7, /device:TPU:1, one launch (start us, length us, event | category | flops | bytes accessed | tf_op | source)
XLA Modules:
  0.0 158.1 jit_solution(3714592660680708602)
XLA Ops:
  6.5 0.0 copy-start
  6.5 0.0 all-gather.2.cloned.1.call-start
  6.5 0.9 convert_reduce_fusion
  7.5 0.1 mul.56
  7.5 0.1 mul.57
  7.6 1.2 copy.9
  8.9 0.8 broadcast_multiply_fusion
  9.7 0.0 all-gather.2.cloned.1.call-update
  9.7 74.1 %all-gather.2.cloned.1.call-done = f32[1024,2048]{0,1:T(8,128)} async-done(((f32[1024,128]{0,1:T(8,128)}), f32[1024,2048]{0,1:T(8,128)}) %all-gather.2.cloned.1.call-update) | async-done | bytes 8388624 | tf_op jit(solution)/shard_map/all_gather | solution.py:42
  83.9 0.8 collective-permute-start
  84.7 0.8 dynamic-slice_convert_fusion
  85.5 0.1 broadcast_in_dim.4
  85.6 0.1 reshape_reshape.3
  85.7 0.0 slice-start
  85.7 0.1 fusion.23
  85.7 0.0 slice-start.1
  85.8 11.9 %fusion.4 = f32[1024,512,1]{1,0,2:T(8,128)S(1)} fusion(f32[1024,16,128]{0,2,1:T(8,128)} %bitcast.71, f32[16,2,128,512]{3,2,1,0:T(8,128)} %bitcast.67, f32[16,512]{1,0:T(8,128)S(1)} %get-tuple-element.7, f32[16,512]{1,0:T(8,128)S(1)} %get-tuple-element.8, pred[]{:T(512)S(6)} %eq.3), kind=kOutput, calls=%fused_computation.6 | convolution fusion | flops 6445596672 | bytes 18939904 | tf_op jit(solution)/shard_map/dot_general | solution.py:50
  97.7 0.1 collective-permute-done
  97.8 0.0 slice-done
  97.8 0.0 slice-done.1
  97.8 10.2 %bitcast_add_fusion = f32[1024,512]{1,0:T(8,128)} fusion(f32[1024,512,1]{1,0,2:T(8,128)S(1)} %fusion.4, f32[1024,16,128]{0,2,1:T(8,128)} %bitcast.4, f32[16,2,128,512]{3,2,1,0:T(8,128)S(1)} %bitcast.70, f32[16,512]{1,0:T(8,128)S(1)} %get-tuple-element.7, f32[16,512]{1,0:T(8,128)S(1)} %get-tuple-element.8, pred[]{:T(512)S(6)} %eq.3), kind=kOutput, calls=%fused_computation.10 | convolution fusion | flops 6446120960 | bytes 21037056 | tf_op jit(solution)/shard_map/dot_general | solution.py:50
  108.1 1.9 %reshape.37 = f32[4,8,32,4,128]{4,3,2,1,0:T(4,128)S(1)} reshape(f32[1024,512]{1,0:T(8,128)} %bitcast_add_fusion) | data formatting | bytes 4194304 | tf_op jit(solution)/shard_map/reshape | solution.py:55
  110.0 1.2 copy.14
  111.2 37.6 %all_to_all.5 = f32[128,8,4,128]{3,1,2,0:T(8,128)S(1)} all-to-all(f32[128,8,4,128]{3,1,2,0:T(8,128)S(1)} %bitcast.64), channel_id=1, replica_groups=mesh['row'=4,'z'=4,'y'=4,'core'=2] {'row','z','y','core'}, dimensions={0} | all-to-all | bytes 4194304 | tf_op jit(solution)/shard_map/all_to_all | solution.py:57
  148.8 0.2 reduce_sum.9
  149.1 0.2 copy.16
  149.3 0.0 copy-done
  149.3 1.0 fusion.20
  150.3 1.0 copy.17
  (2 shorter events, 0.0 us)
Async XLA Ops:
  6.5 142.8 %copy-start = (f32[128,128]{1,0:T(8,128)S(1)}, f32[128,128]{1,0:T(8,128)}, u32[]{:S(2)}) copy-start(f32[128,128]{1,0:T(8,128)} %param.7) | copy-start | bytes 196612
  6.5 77.3 %all-gather.2.cloned.1.call-start = ((), (), s32[]{:S(2)}) async-start(), calls=%async_computation.1 | async-start | bytes 8912896 | tf_op jit(solution)/shard_map/all_gather | solution.py:42
  83.9 14.0 %collective-permute-start = (f32[1024,2048]{0,1:T(8,128)}, f32[1024,2048]{0,1:T(8,128)}, u32[]{:S(2)}, u32[]{:S(2)}) collective-permute-start(f32[1024,2048]{0,1:T(8,128)} %all-gather.2.cloned.1.call-done), channel_id=1, source_target_pairs={{0,1},{1,0},{2,3},{3,2},{4,5},{5,4},{6,7},{7,6},{8,9},{9,8},{10,11... | collective-permute-start | bytes 25165832 | tf_op jit(solution)/shard_map/ppermute | solution.py:43
  85.7 12.2 %slice-start = ((s8[8388608]{0:T(1024)(128)(4,1)}), s8[4194304]{0:T(1024)(128)(4,1)S(1)}, s32[]{:S(2)}) async-start(s8[8388608]{0:T(1024)(128)(4,1)} %bitcast.68), calls=%async_computation.2 | async-start | bytes 8388608
  85.7 12.1 %slice-start.1 = ((s8[8388608]{0:T(1024)(128)(4,1)}), s8[4194304]{0:T(1024)(128)(4,1)S(1)}, s32[]{:S(2)}) async-start(s8[8388608]{0:T(1024)(128)(4,1)} %bitcast.68), calls=%async_computation.3 | async-start | bytes 8388608
Sparse Core Ops, SparseCore 0:
  9.9 73.9 all-gather.1

commit v8 on v7

--- a/solution.py
+++ b/solution.py
@@ -47,15 +47,20 @@
     own = own.reshape(pairs, n_zy, k_local)
     other = other.reshape(pairs, n_zy, k_local)
     dims = (((1, 2), (0, 1)), ((), ()))
-    partial = lax.dot_general(own, ints_own, dims, precision=lax.Precision.HIGH) + lax.dot_general(
-        other, ints_other, dims, precision=lax.Precision.HIGH
-    )
 
     i_local = pairs // n_row // occ_j
-    buf = partial.reshape(n_row, i_local, occ_j, a_cols, virt).transpose(0, 2, 1, 3, 4)
-    buf = buf.reshape(n_row * occ_j, i_local, a_cols, virt)
-    recv = lax.all_to_all(buf, ("row",) + COL, split_axis=0, concat_axis=0, tiled=True)
-    summed = recv.reshape(n_row, n_col, i_local, a_cols, virt).sum(axis=0)
+    n_half = n_local // 2
+    halves = []
+    for h in range(2):
+        cols = slice(h * n_half, (h + 1) * n_half)
+        partial = lax.dot_general(
+            own, ints_own[..., cols], dims, precision=lax.Precision.HIGH
+        ) + lax.dot_general(other, ints_other[..., cols], dims, precision=lax.Precision.HIGH)
+        buf = partial.reshape(n_row, i_local, occ_j, n_half).transpose(0, 2, 1, 3)
+        buf = buf.reshape(n_row * occ_j, i_local, n_half)
+        recv = lax.all_to_all(buf, ("row",) + COL, split_axis=0, concat_axis=0, tiled=True)
+        halves.append(recv.reshape(n_row, n_col, i_local, n_half).sum(axis=0))
+    summed = jnp.stack(halves, axis=2)
     block = summed.transpose(1, 0, 2, 3).reshape(i_local, 1, n_col * a_cols, virt)
     return block + jnp.einsum("ac,ijcb->ijab", vv_coupling, block, precision=lax.Precision.HIGHEST)
 

time: 158 us -> 178 us (1.13)
  blocking collectives: 37.6 us -> 0 us
  waiting for transfers between devices: 74.3 us -> 93.1 us
  starting transfers between devices: 0.84 us -> 17.9 us
  matrix products: 23.2 us -> 36.7 us
  other arithmetic: 2.81 us -> 7.61 us
  local copies, waits for them, and re-layouts: 5.99 us -> 8.37 us
    all_to_all x1 -> x0, blocking collectives: 37.6 us -> none  [body(): lax.all_to_all(buf, ('row',) + COL, split_axis=0, concat_axis=0, tiled=True)]
    all_to_all x0 -> x2, waiting for transfers between devices: none -> 18.9 us  [body(): lax.all_to_all(buf, ('row',) + COL, split_axis=0, concat_axis=0, tiled=True)]
    all_to_all x0 -> x2, starting transfers between devices: none -> 17.1 us  [body(): lax.all_to_all(buf, ('row',) + COL, split_axis=0, concat_axis=0, tiled=True)]
    dot_general x2 -> x4, matrix products: 22.2 us -> 35.7 us  [the longest x2 18.8 us: body(): lax.dot_general(other, ints_other[..., cols], dims, precision=lax.Precisi...]
    select_n x0 -> x1, other arithmetic: none -> 4.85 us  [body(): ints_other = jnp.where(first, ints_c1, ints_c0)]
    reshape x2 -> x3, local copies, waits for them, and re-layouts: 3.15 us -> 3.69 us  [the longest x2 3.27 us: body(): buf = partial.reshape(n_row, i_local, occ_j, n_half).transpose(0, 2, 1, 3)]
  transfers between devices with their start and end apart: 2 -> 4, of which waited for: 2 -> 2; matrix products, arithmetic and copies ran while one was open for 8% -> 19% of each run, Pallas kernels for 0% -> 0%
where the time goes in v8:
time: 178 us; the launch traced here: 177 us
  waiting for transfers between devices  93.1 us (52%)
  matrix products  36.7 us (21%)
  starting transfers between devices  17.9 us (10%)
  between operations  13.6 us (8%)
  local copies, waits for them, and re-layouts  8.37 us (5%)
  other arithmetic  7.61 us (4%)
    all_gather x1, waiting for transfers between devices, body(): own = lax.all_gather(amp_screened, PLANE, axis=1, tiled=True)  74.1 us
    all_to_all x2, waiting for transfers between devices, body(): lax.all_to_all(buf, ('row',) + COL, split_axis=0, concat_axis=0, tiled=True)  18.9 us
    dot_general x2, matrix products, body(): lax.dot_general(other, ints_other[..., cols], dims, precision=lax.Precisi...  18.8 us
    all_to_all x2, starting transfers between devices, body(): lax.all_to_all(buf, ('row',) + COL, split_axis=0, concat_axis=0, tiled=True)  17.1 us
    dot_general x2, matrix products, body(): lax.dot_general(own, ints_own[..., cols], dims, precision=lax.Precision.H...  16.9 us
    select_n x1, other arithmetic, body(): ints_other = jnp.where(first, ints_c1, ints_c0)  4.85 us
  transfers between devices with their start and end apart: 4, of which 2 were waited for; matrix products, arithmetic and copies ran while one was open for 19% of the time, Pallas kernels for 0%

profile of v8, /device:TPU:1, one launch (start us, length us, event | category | flops | bytes accessed | tf_op | source)
XLA Modules:
  0.0 177.3 jit_solution(7025569422726125047)
XLA Ops:
  6.5 0.9 convert_reduce_fusion
  7.5 0.1 mul.52
  7.5 0.1 mul.53
  7.6 1.2 copy.19
  8.9 0.8 broadcast_multiply_fusion
  9.7 0.0 all-gather.2.cloned.1.call-update
  9.7 74.1 %all-gather.2.cloned.1.call-done = f32[1024,2048]{0,1:T(8,128)} async-done(((f32[1024,128]{0,1:T(8,128)}), f32[1024,2048]{0,1:T(8,128)}) %all-gather.2.cloned.1.call-update) | async-done | bytes 8388624 | tf_op jit(solution)/shard_map/all_gather | solution.py:42
  83.9 0.8 collective-permute-start
  84.7 0.8 dynamic-slice_convert_fusion
  85.5 0.1 broadcast_in_dim.4
  85.6 0.1 reshape_reshape.3
  85.7 0.1 fusion.32
  85.7 0.0 slice-start
  85.8 4.9 %fusion.2 = (f32[16,128,512]{2,1,0:T(8,128)S(1)}, f32[16,128,512]{2,1,0:T(8,128)S(1)}) fusion(f32[16,2,128,512]{3,2,1,0:T(8,128)} %bitcast.71, f32[16,512]{1,0:T(8,128)S(1)} %get-tuple-element.9, f32[16,512]{1,0:T(8,128)S(1)} %get-tuple-element.10, pred[]{:T(512)S(6)} %eq.3), kind=kLoop, calls=%fused_computation.4 | loop fusion | flops 4194304 | bytes 16842752 | tf_op jit(solution)/shard_map/jit(_where)/select_n | solution.py:46
  90.6 1.0 slice-done.1
  91.7 7.0 %fusion.18 = f32[1024,256]{1,0:T(8,128)S(1)} fusion(f32[1024,16,128]{0,2,1:T(8,128)S(1)} %bitcast.70, f32[16,128,512]{2,1,0:T(8,128)S(1)} %get-tuple-element.6), kind=kOutput, calls=%fused_computation.16 | convolution fusion | flops 3221225472 | bytes 11534336 | tf_op jit(solution)/shard_map/dot_general | solution.py:56
  98.7 9.4 %fusion.24 = f32[1024,256]{1,0:T(8,128)S(1)} fusion(f32[1024,256]{1,0:T(8,128)S(1)} %fusion.18, f32[1024,16,128]{0,2,1:T(8,128)} %bitcast.5, f32[16,128,512]{2,1,0:T(8,128)S(1)} %get-tuple-element.5), kind=kOutput, calls=%fused_computation.18 | convolution fusion | flops 3221487616 | bytes 12582912 | tf_op jit(solution)/shard_map/dot_general | solution.py:58
  108.1 1.7 copy.27
  109.8 7.3 %all-to-all-start.1 = ((f32[128,8,256]{2,1,0:T(8,128)}), f32[128,8,256]{2,1,0:T(8,128)S(1)}, u32[]{:S(2)}, u32[]{:S(2)}) async-start(f32[128,8,256]{2,1,0:T(8,128)} %bitcast.16), calls=%async_computation.1 | async-start | bytes 2097152 | tf_op jit(solution)/shard_map/all_to_all | solution.py:61
  117.1 9.9 %fusion.12 = f32[1024,256]{1,0:T(8,128)S(1)} fusion(f32[1024,16,128]{0,2,1:T(8,128)} %bitcast.67, f32[16,128,512]{2,1,0:T(8,128)} %copy-done.1), kind=kOutput, calls=%fused_computation.14 | convolution fusion | flops 3221225472 | bytes 11534336 | tf_op jit(solution)/shard_map/dot_general | solution.py:56
  127.1 9.4 %fusion.27 = f32[1024,256]{1,0:T(8,128)S(1)} fusion(f32[1024,256]{1,0:T(8,128)S(1)} %fusion.12, f32[1024,16,128]{0,2,1:T(8,128)} %bitcast.5, f32[16,128,512]{2,1,0:T(8,128)S(1)} %copy-done.3), kind=kOutput, calls=%fused_computation.19 | convolution fusion | flops 3221487616 | bytes 12582912 | tf_op jit(solution)/shard_map/dot_general | solution.py:58
  136.5 1.6 copy.24
  138.0 9.8 %all-to-all-start = ((f32[128,8,256]{2,1,0:T(8,128)}), f32[128,8,256]{2,1,0:T(8,128)S(1)}, u32[]{:S(2)}, u32[]{:S(2)}) async-start(f32[128,8,256]{2,1,0:T(8,128)} %bitcast.9), calls=%async_computation | async-start | bytes 2097152 | tf_op jit(solution)/shard_map/all_to_all | solution.py:61
  147.8 0.1 reduce_sum.19
  147.9 18.9 %all-to-all-done = f32[128,8,256]{2,1,0:T(8,128)S(1)} async-done(((f32[128,8,256]{2,1,0:T(8,128)}), f32[128,8,256]{2,1,0:T(8,128)S(1)}, u32[]{:S(2)}, u32[]{:S(2)}) %all-to-all-start) | async-done | bytes 1048608 | tf_op jit(solution)/shard_map/all_to_all | solution.py:61
  166.8 0.1 reduce_sum.18
  167.0 0.4 copy.28
  167.4 0.4 reshape.51
  167.8 0.4 reshape.50
  168.2 0.2 copy.31
  168.4 1.0 fusion.30
  169.4 1.0 copy.32
  (16 shorter events, 0.1 us)
Async XLA Ops:
  6.5 161.9 %copy-start = (f32[128,128]{1,0:T(8,128)S(1)}, f32[128,128]{1,0:T(8,128)}, u32[]{:S(2)}) copy-start(f32[128,128]{1,0:T(8,128)} %param.7) | copy-start | bytes 196612
  6.5 77.3 %all-gather.2.cloned.1.call-start = ((), (), s32[]{:S(2)}) async-start(), calls=%async_computation.2 | async-start | bytes 8912896 | tf_op jit(solution)/shard_map/all_gather | solution.py:42
  83.9 14.8 %collective-permute-start = (f32[1024,2048]{0,1:T(8,128)}, f32[1024,2048]{0,1:T(8,128)}, u32[]{:S(2)}, u32[]{:S(2)}) collective-permute-start(f32[1024,2048]{0,1:T(8,128)} %all-gather.2.cloned.1.call-done), channel_id=1, source_target_pairs={{0,1},{1,0},{2,3},{3,2},{4,5},{5,4},{6,7},{7,6},{8,9},{9,8},{10,11... | collective-permute-start | bytes 25165832 | tf_op jit(solution)/shard_map/ppermute | solution.py:43
  85.7 4.9 %slice-start = ((s8[8388608]{0:T(1024)(128)(4,1)}), s8[4194304]{0:T(1024)(128)(4,1)S(1)}, s32[]{:S(2)}) async-start(s8[8388608]{0:T(1024)(128)(4,1)} %bitcast.68), calls=%async_computation.3 | async-start | bytes 8388608
  85.7 5.9 %slice-start.1 = ((s8[8388608]{0:T(1024)(128)(4,1)}), s8[4194304]{0:T(1024)(128)(4,1)S(1)}, s32[]{:S(2)}) async-start(s8[8388608]{0:T(1024)(128)(4,1)} %bitcast.68), calls=%async_computation.4 | async-start | bytes 8388608
  90.6 8.1 %copy-start.1 = (f32[16,128,512]{2,1,0:T(8,128)}, f32[16,128,512]{2,1,0:T(8,128)S(1)}, u32[]{:S(2)}) copy-start(f32[16,128,512]{2,1,0:T(8,128)S(1)} %get-tuple-element.6) | copy-start | bytes 12582916
  90.6 8.1 %copy-start.2 = (f32[16,128,512]{2,1,0:T(8,128)}, f32[16,128,512]{2,1,0:T(8,128)S(1)}, u32[]{:S(2)}) copy-start(f32[16,128,512]{2,1,0:T(8,128)S(1)} %get-tuple-element.5) | copy-start | bytes 12582916
  109.8 28.2 %all-to-all-start.1 = ((f32[128,8,256]{2,1,0:T(8,128)}), f32[128,8,256]{2,1,0:T(8,128)S(1)}, u32[]{:S(2)}, u32[]{:S(2)}) async-start(f32[128,8,256]{2,1,0:T(8,128)} %bitcast.16), calls=%async_computation.1 | async-start | bytes 2097152 | tf_op jit(solution)/shard_map/all_to_all | solution.py:61
  117.1 9.9 %copy-start.3 = (f32[16,128,512]{2,1,0:T(8,128)S(1)}, f32[16,128,512]{2,1,0:T(8,128)}, u32[]{:S(2)}) copy-start(f32[16,128,512]{2,1,0:T(8,128)} %copy-done.2) | copy-start | bytes 12582916
  138.0 28.8 %all-to-all-start = ((f32[128,8,256]{2,1,0:T(8,128)}), f32[128,8,256]{2,1,0:T(8,128)S(1)}, u32[]{:S(2)}, u32[]{:S(2)}) async-start(f32[128,8,256]{2,1,0:T(8,128)} %bitcast.9), calls=%async_computation | async-start | bytes 2097152 | tf_op jit(solution)/shard_map/all_to_all | solution.py:61
Sparse Core Ops, SparseCore 0:
  9.9 73.9 all-gather.1

commit v9 on v7

--- a/solution.py
+++ b/solution.py
@@ -56,8 +56,9 @@
     buf = buf.reshape(n_row * occ_j, i_local, a_cols, virt)
     recv = lax.all_to_all(buf, ("row",) + COL, split_axis=0, concat_axis=0, tiled=True)
     summed = recv.reshape(n_row, n_col, i_local, a_cols, virt).sum(axis=0)
-    block = summed.transpose(1, 0, 2, 3).reshape(i_local, 1, n_col * a_cols, virt)
-    return block + jnp.einsum("ac,ijcb->ijab", vv_coupling, block, precision=lax.Precision.HIGHEST)
+    dressing = (jnp.eye(virt, dtype=vv_coupling.dtype) + vv_coupling).reshape(virt, n_col, a_cols)
+    out = jnp.einsum("akc,kicb->iab", dressing, summed, precision=lax.Precision.HIGHEST)
+    return out.reshape(i_local, 1, virt, virt)
 
 
 def solution(mesh):

time: 158 us -> 160 us (1.013)
  blocking collectives: 37.6 us -> 0 us
  waiting for transfers between devices: 74.3 us -> 104 us
  starting transfers between devices: 0.84 us -> 8.4 us
    all_to_all x1 -> x0, blocking collectives: 37.6 us -> none  [body(): lax.all_to_all(buf, ('row',) + COL, split_axis=0, concat_axis=0, tiled=True)]
    all_to_all x0 -> x1, waiting for transfers between devices: none -> 30.1 us  [body(): lax.all_to_all(buf, ('row',) + COL, split_axis=0, concat_axis=0, tiled=True)]
    all_to_all x0 -> x1, starting transfers between devices: none -> 7.56 us  [body(): lax.all_to_all(buf, ('row',) + COL, split_axis=0, concat_axis=0, tiled=True)]
  transfers between devices with their start and end apart: 2 -> 3, of which waited for: 2 -> 3; matrix products, arithmetic and copies ran while one was open for 8% -> 8% of each run, Pallas kernels for 0% -> 0%
where the time goes in v9:
time: 160 us
  waiting for transfers between devices  104 us (65%)
  matrix products  23.3 us (15%)
  between operations  13.5 us (8%)
  starting transfers between devices  8.4 us (5%)
  local copies, waits for them, and re-layouts  7.2 us (4%)
  other arithmetic  2.79 us (2%)
    all_gather x1, waiting for transfers between devices, body(): own = lax.all_gather(amp_screened, PLANE, axis=1, tiled=True)  74.1 us
    all_to_all x1, waiting for transfers between devices, body(): lax.all_to_all(buf, ('row',) + COL, split_axis=0, concat_axis=0, tiled=True)  30.1 us
    dot_general x1, matrix products, body(): lax.dot_general(own, ints_own, dims, precision=lax.Precision.HIGH)  11.9 us
    dot_general x1, matrix products, body(): lax.dot_general(other, ints_other, dims, precision=lax.Precision.HIGH)  10.2 us
    all_to_all x1, starting transfers between devices, body(): lax.all_to_all(buf, ('row',) + COL, split_axis=0, concat_axis=0, tiled=True)  7.56 us
    reshape x2, local copies, waits for them, and re-layouts, body(): partial.reshape(n_row, i_local, occ_j, a_cols, virt)  4.5 us
  transfers between devices with their start and end apart: 3, of which 3 were waited for; matrix products, arithmetic and copies ran while one was open for 8% of the time, Pallas kernels for 0%

profile of v9, /device:TPU:1, one launch (start us, length us, event | category | flops | bytes accessed | tf_op | source)
XLA Modules:
  0.0 159.6 jit_solution(16932260377010731309)
XLA Ops:
  6.5 0.0 all-gather.2.cloned.1.call-start
  6.5 0.9 convert_reduce_fusion
  7.4 0.1 mul.56
  7.5 0.1 mul.57
  7.6 1.2 copy.19
  8.8 0.8 broadcast_multiply_fusion
  9.7 0.0 all-gather.2.cloned.1.call-update
  9.7 74.1 %all-gather.2.cloned.1.call-done = f32[1024,2048]{0,1:T(8,128)} async-done(((f32[1024,128]{0,1:T(8,128)}), f32[1024,2048]{0,1:T(8,128)}) %all-gather.2.cloned.1.call-update) | async-done | bytes 8388624 | tf_op jit(solution)/shard_map/all_gather | solution.py:42
  83.8 0.8 collective-permute-start
  84.7 0.8 dynamic-slice_convert_fusion
  85.5 0.1 broadcast_in_dim.4
  85.6 0.1 reshape_reshape.3
  85.6 0.0 slice-start
  85.6 0.1 fusion.23
  85.7 0.0 slice-start.1
  85.7 11.9 %fusion.4 = f32[1024,512,1]{1,0,2:T(8,128)S(1)} fusion(f32[1024,16,128]{0,2,1:T(8,128)} %bitcast.67, f32[16,2,128,512]{3,2,1,0:T(8,128)} %bitcast.63, f32[16,512]{1,0:T(8,128)S(1)} %get-tuple-element.7, f32[16,512]{1,0:T(8,128)S(1)} %get-tuple-element.8, pred[]{:T(512)S(6)} %eq.6), kind=kOutput, calls=%fused_computation.6 | convolution fusion | flops 6445596672 | bytes 18939904 | tf_op jit(solution)/shard_map/dot_general | solution.py:50
  97.7 0.1 collective-permute-done
  97.8 0.0 slice-done
  97.8 0.0 slice-done.1
  97.8 10.2 %bitcast_add_fusion = f32[1024,512]{1,0:T(8,128)} fusion(f32[1024,512,1]{1,0,2:T(8,128)S(1)} %fusion.4, f32[1024,16,128]{0,2,1:T(8,128)} %bitcast.4, f32[16,2,128,512]{3,2,1,0:T(8,128)S(1)} %bitcast.66, f32[16,512]{1,0:T(8,128)S(1)} %get-tuple-element.7, f32[16,512]{1,0:T(8,128)S(1)} %get-tuple-element.8, pred[]{:T(512)S(6)} %eq.6), kind=kOutput, calls=%fused_computation.10 | convolution fusion | flops 6446120960 | bytes 21037056 | tf_op jit(solution)/shard_map/dot_general | solution.py:50
  108.0 1.9 %reshape.35 = f32[4,8,32,4,128]{4,3,2,1,0:T(4,128)S(1)} reshape(f32[1024,512]{1,0:T(8,128)} %bitcast_add_fusion) | data formatting | bytes 4194304 | tf_op jit(solution)/shard_map/reshape | solution.py:55
  110.0 0.0 copy-start
  110.0 2.6 %copy.24 = f32[4,8,32,4,128]{4,1,3,2,0:T(8,128)} copy(f32[4,8,32,4,128]{4,3,2,1,0:T(4,128)S(1)} %reshape.35) | data formatting | bytes 4194304 | tf_op jit(solution)/shard_map/reshape | solution.py:55
  112.6 7.6 %all-to-all-start = ((f32[128,8,4,128]{3,1,2,0:T(8,128)}), f32[128,8,4,128]{3,1,2,0:T(8,128)S(1)}, u32[]{:S(2)}, u32[]{:S(2)}) async-start(f32[128,8,4,128]{3,1,2,0:T(8,128)} %bitcast.61), calls=%async_computation | async-start | bytes 4194304 | tf_op jit(solution)/shard_map/all_to_all | solution.py:57
  120.1 0.0 copy-done
  120.1 0.1 copy.25
  120.3 30.1 %all-to-all-done = f32[128,8,4,128]{3,1,2,0:T(8,128)S(1)} async-done(((f32[128,8,4,128]{3,1,2,0:T(8,128)}), f32[128,8,4,128]{3,1,2,0:T(8,128)S(1)}, u32[]{:S(2)}, u32[]{:S(2)}) %all-to-all-start) | async-done | bytes 2097184 | tf_op jit(solution)/shard_map/all_to_all | solution.py:57
  150.3 0.2 reduce_sum.9
  150.6 1.2 convolution_bitcast_fusion
  151.8 1.0 copy.28
  (3 shorter events, 0.0 us)
Async XLA Ops:
  6.5 77.3 %all-gather.2.cloned.1.call-start = ((), (), s32[]{:S(2)}) async-start(), calls=%async_computation.1 | async-start | bytes 8912896 | tf_op jit(solution)/shard_map/all_gather | solution.py:42
  83.8 14.0 %collective-permute-start = (f32[1024,2048]{0,1:T(8,128)}, f32[1024,2048]{0,1:T(8,128)}, u32[]{:S(2)}, u32[]{:S(2)}) collective-permute-start(f32[1024,2048]{0,1:T(8,128)} %all-gather.2.cloned.1.call-done), channel_id=1, source_target_pairs={{0,1},{1,0},{2,3},{3,2},{4,5},{5,4},{6,7},{7,6},{8,9},{9,8},{10,11... | collective-permute-start | bytes 25165832 | tf_op jit(solution)/shard_map/ppermute | solution.py:43
  85.6 12.2 %slice-start = ((s8[8388608]{0:T(1024)(128)(4,1)}), s8[4194304]{0:T(1024)(128)(4,1)S(1)}, s32[]{:S(2)}) async-start(s8[8388608]{0:T(1024)(128)(4,1)} %bitcast.64), calls=%async_computation.2 | async-start | bytes 8388608
  85.7 12.1 %slice-start.1 = ((s8[8388608]{0:T(1024)(128)(4,1)}), s8[4194304]{0:T(1024)(128)(4,1)S(1)}, s32[]{:S(2)}) async-start(s8[8388608]{0:T(1024)(128)(4,1)} %bitcast.64), calls=%async_computation.3 | async-start | bytes 8388608
  110.0 10.2 %copy-start = (f32[128,128]{1,0:T(8,128)S(1)}, f32[128,128]{1,0:T(8,128)}, u32[]{:S(2)}) copy-start(f32[128,128]{1,0:T(8,128)} %param.7) | copy-start | bytes 196612
  112.6 37.8 %all-to-all-start = ((f32[128,8,4,128]{3,1,2,0:T(8,128)}), f32[128,8,4,128]{3,1,2,0:T(8,128)S(1)}, u32[]{:S(2)}, u32[]{:S(2)}) async-start(f32[128,8,4,128]{3,1,2,0:T(8,128)} %bitcast.61), calls=%async_computation | async-start | bytes 4194304 | tf_op jit(solution)/shard_map/all_to_all | solution.py:57
Sparse Core Ops, SparseCore 0:
  9.8 73.9 all-gather.1

commit v10 on v7

--- a/solution.py
+++ b/solution.py
@@ -1,6 +1,7 @@
 import jax
 import jax.numpy as jnp
 from jax import lax
+from jax.experimental.layout import Layout, with_layout_constraint
 from jax.sharding import Mesh
 from jax.sharding import PartitionSpec as P
 
@@ -23,9 +24,10 @@
 
     c_own = row_id * n_col + col_id
     amp_col = lax.dynamic_slice_in_dim(amp_mask, c_own, 1, axis=1).astype(jnp.float32)
-    amp_screened = (amplitudes.reshape(occ_i, occ_j, k_local) * amp_col[:, :, None]).reshape(
-        pairs, k_local
-    )
+    i_local = occ_i // n_row
+    amp_screened = amplitudes.reshape(occ_i, occ_j, k_local) * amp_col[:, :, None]
+    amp_t = amp_screened.reshape(n_row, i_local, occ_j, k_local).transpose(3, 0, 2, 1)
+    amp_t = with_layout_constraint(amp_t.reshape(k_local, pairs), Layout((0, 1)))
 
     c_rows = virt // n_row
     a_cols = virt // n_col
@@ -39,21 +41,19 @@
     ints_c0 = ints[:, 0] * masks[:, 0]
     ints_c1 = ints[:, 1] * masks[:, 1]
 
-    own = lax.all_gather(amp_screened, PLANE, axis=1, tiled=True)
+    own = with_layout_constraint(lax.all_gather(amp_t, PLANE, axis=0, tiled=True), Layout((0, 1)))
     other = lax.ppermute(own, "core", [(0, 1), (1, 0)])
     first = core_id == 0
     ints_own = jnp.where(first, ints_c0, ints_c1)
     ints_other = jnp.where(first, ints_c1, ints_c0)
-    own = own.reshape(pairs, n_zy, k_local)
-    other = other.reshape(pairs, n_zy, k_local)
-    dims = (((1, 2), (0, 1)), ((), ()))
+    own = own.reshape(n_zy, k_local, pairs)
+    other = other.reshape(n_zy, k_local, pairs)
+    dims = (((0, 1), (0, 1)), ((), ()))
     partial = lax.dot_general(own, ints_own, dims, precision=lax.Precision.HIGH) + lax.dot_general(
         other, ints_other, dims, precision=lax.Precision.HIGH
     )
 
-    i_local = pairs // n_row // occ_j
-    buf = partial.reshape(n_row, i_local, occ_j, a_cols, virt).transpose(0, 2, 1, 3, 4)
-    buf = buf.reshape(n_row * occ_j, i_local, a_cols, virt)
+    buf = partial.reshape(n_row * occ_j, i_local, a_cols, virt)
     recv = lax.all_to_all(buf, ("row",) + COL, split_axis=0, concat_axis=0, tiled=True)
     summed = recv.reshape(n_row, n_col, i_local, a_cols, virt).sum(axis=0)
     block = summed.transpose(1, 0, 2, 3).reshape(i_local, 1, n_col * a_cols, virt)

time: 158 us -> 155 us (0.981)
  local copies, waits for them, and re-layouts: 5.99 us -> 2.83 us
    reshape x2 -> x1, local copies, waits for them, and re-layouts: 3.15 us -> 1 us  [body(): amp_t.reshape(k_local, pairs)]
where the time goes in v10:
time: 155 us; the launch traced here: 154 us
  waiting for transfers between devices  74.3 us (48%)
  blocking collectives  37.6 us (24%)
  matrix products  22.2 us (14%)
  between operations  13.5 us (9%)
  other arithmetic  3.11 us (2%)
  local copies, waits for them, and re-layouts  2.83 us (2%)
    all_gather x1, waiting for transfers between devices, body(): lax.all_gather(amp_t, PLANE, axis=0, tiled=True)  74.1 us
    all_to_all x1, blocking collectives, body(): lax.all_to_all(buf, ('row',) + COL, split_axis=0, concat_axis=0, tiled=True)  37.6 us
    dot_general x1, matrix products, body(): lax.dot_general(own, ints_own, dims, precision=lax.Precision.HIGH)  11.9 us
    dot_general x1, matrix products, body(): lax.dot_general(other, ints_other, dims, precision=lax.Precision.HIGH)  9.3 us
  transfers between devices with their start and end apart: 2, of which 2 were waited for; matrix products, arithmetic and copies ran while one was open for 8% of the time, Pallas kernels for 0%

profile of v10, /device:TPU:1, one launch (start us, length us, event | category | flops | bytes accessed | tf_op | source)
XLA Modules:
  0.0 154.3 jit_solution(10399664096158995667)
XLA Ops:
  6.5 0.0 copy-start
  6.5 0.0 all-gather.2.cloned.1.call-start
  6.5 0.9 convert_reduce_fusion
  7.5 0.1 mul.51
  7.6 1.1 multiply_bitcast_fusion
  8.7 0.3 copy.18
  9.0 1.0 copy.19
  10.0 0.0 all-gather.2.cloned.1.call-update
  10.0 74.1 %all-gather.2.cloned.1.call-done = f32[2048,1024]{1,0:T(8,128)} async-done(((f32[128,1024]{1,0:T(8,128)}), f32[2048,1024]{1,0:T(8,128)}) %all-gather.2.cloned.1.call-update) | async-done | bytes 8388624 | tf_op jit(solution)/shard_map/all_gather | solution.py:44
  84.2 0.8 collective-permute-start
  85.0 0.8 dynamic-slice_convert_fusion
  85.8 0.1 broadcast_in_dim.4
  85.9 0.1 reshape_reshape.3
  86.0 0.0 slice-start
  86.0 0.1 fusion.24
  86.1 0.0 slice-start.1
  86.1 11.9 %fusion.4 = f32[1024,512,1]{1,0,2:T(8,128)S(1)} fusion(f32[16,128,1024]{2,1,0:T(8,128)} %bitcast.77, f32[16,2,128,512]{3,2,1,0:T(8,128)} %bitcast.73, f32[16,512]{1,0:T(8,128)S(1)} %get-tuple-element.7, f32[16,512]{1,0:T(8,128)S(1)} %get-tuple-element.8, pred[]{:T(512)S(6)} %eq.3), kind=kOutput, calls=%fused_computation.6 | convolution fusion | flops 6445596672 | bytes 18939904 | tf_op jit(solution)/shard_map/dot_general | solution.py:52
  98.0 0.2 collective-permute-done
  98.1 0.0 slice-done
  98.1 0.0 slice-done.1
  98.1 9.3 %fusion.12 = f32[128,8,4,128]{3,1,2,0:T(8,128)S(1)} fusion(f32[1024,512,1]{1,0,2:T(8,128)S(1)} %fusion.4, f32[16,128,1024]{2,1,0:T(8,128)} %bitcast.7, f32[16,2,128,512]{3,2,1,0:T(8,128)S(1)} %bitcast.76, f32[16,512]{1,0:T(8,128)S(1)} %get-tuple-element.7, f32[16,512]{1,0:T(8,128)S(1)} %get-tuple-element.8, pred[]{:T(512)S(6)} %eq.3), kind=kOutput, calls=%fused_computation.11 | convolution fusion | flops 6446120960 | bytes 21037056 | tf_op jit(solution)/shard_map/dot_general | solution.py:52
  107.4 37.6 %all_to_all.5 = f32[128,8,4,128]{3,1,2,0:T(8,128)S(1)} all-to-all(f32[128,8,4,128]{3,1,2,0:T(8,128)S(1)} %fusion.12), channel_id=1, replica_groups=mesh['row'=4,'z'=4,'y'=4,'core'=2] {'row','z','y','core'}, dimensions={0} | all-to-all | bytes 4194304 | tf_op jit(solution)/shard_map/all_to_all | solution.py:57
  145.0 0.2 reduce_sum.9
  145.3 0.2 copy.24
  145.5 0.0 copy-done
  145.5 1.0 fusion.21
  146.5 1.0 copy.25
  (2 shorter events, 0.0 us)
Async XLA Ops:
  6.5 139.0 %copy-start = (f32[128,128]{1,0:T(8,128)S(1)}, f32[128,128]{1,0:T(8,128)}, u32[]{:S(2)}) copy-start(f32[128,128]{1,0:T(8,128)} %param.7) | copy-start | bytes 196612
  6.5 77.6 %all-gather.2.cloned.1.call-start = ((), (), s32[]{:S(2)}) async-start(), calls=%async_computation.1 | async-start | bytes 8912896 | tf_op jit(solution)/shard_map/all_gather | solution.py:44
  84.2 14.0 %collective-permute-start = (f32[2048,1024]{1,0:T(8,128)}, f32[2048,1024]{1,0:T(8,128)}, u32[]{:S(2)}, u32[]{:S(2)}) collective-permute-start(f32[2048,1024]{1,0:T(8,128)} %all-gather.2.cloned.1.call-done), channel_id=1, source_target_pairs={{0,1},{1,0},{2,3},{3,2},{4,5},{5,4},{6,7},{7,6},{8,9},{9,8},{10,11... | collective-permute-start | bytes 25165832 | tf_op jit(solution)/shard_map/ppermute | solution.py:45
  86.0 12.2 %slice-start = ((s8[8388608]{0:T(1024)(128)(4,1)}), s8[4194304]{0:T(1024)(128)(4,1)S(1)}, s32[]{:S(2)}) async-start(s8[8388608]{0:T(1024)(128)(4,1)} %bitcast.74), calls=%async_computation.2 | async-start | bytes 8388608
  86.1 12.1 %slice-start.1 = ((s8[8388608]{0:T(1024)(128)(4,1)}), s8[4194304]{0:T(1024)(128)(4,1)S(1)}, s32[]{:S(2)}) async-start(s8[8388608]{0:T(1024)(128)(4,1)} %bitcast.74), calls=%async_computation.3 | async-start | bytes 8388608
Sparse Core Ops, SparseCore 0:
  10.2 73.9 all-gather.1

commit v11 on v10

--- a/solution.py
+++ b/solution.py
@@ -3,6 +3,7 @@
 from jax import lax
 from jax.experimental.layout import Layout, with_layout_constraint
 from jax.sharding import Mesh
+
 from jax.sharding import PartitionSpec as P
 
 PLANE = ("z", "y")
@@ -41,11 +42,13 @@
     ints_c0 = ints[:, 0] * masks[:, 0]
     ints_c1 = ints[:, 1] * masks[:, 1]
 
-    own = with_layout_constraint(lax.all_gather(amp_t, PLANE, axis=0, tiled=True), Layout((0, 1)))
+    own = lax.all_gather(amp_t, PLANE, axis=0, tiled=True)
+    own = with_layout_constraint(own, Layout((0, 1)))
     other = lax.ppermute(own, "core", [(0, 1), (1, 0)])
     first = core_id == 0
     ints_own = jnp.where(first, ints_c0, ints_c1)
     ints_other = jnp.where(first, ints_c1, ints_c0)
+    ints_own, ints_other = lax.optimization_barrier((ints_own, ints_other))
     own = own.reshape(n_zy, k_local, pairs)
     other = other.reshape(n_zy, k_local, pairs)
     dims = (((0, 1), (0, 1)), ((), ()))
@@ -57,7 +60,10 @@
     recv = lax.all_to_all(buf, ("row",) + COL, split_axis=0, concat_axis=0, tiled=True)
     summed = recv.reshape(n_row, n_col, i_local, a_cols, virt).sum(axis=0)
     block = summed.transpose(1, 0, 2, 3).reshape(i_local, 1, n_col * a_cols, virt)
-    return block + jnp.einsum("ac,ijcb->ijab", vv_coupling, block, precision=lax.Precision.HIGHEST)
+    row_major = Layout((0, 1, 2, 3))
+    block = with_layout_constraint(block, row_major)
+    out = block + jnp.einsum("ac,ijcb->ijab", vv_coupling, block, precision=lax.Precision.HIGHEST)
+    return with_layout_constraint(out, row_major)
 
 
 def solution(mesh):
@@ -66,4 +72,5 @@
     mesh3 = Mesh(mesh.devices.reshape(n_row, n_side, n_col // 2 // n_side, 2), ("row",) + COL)
     in_specs = (P(None, ("row",) + COL), P("row", COL), P(), P(), P())
     out_specs = P("row", COL, None, None)
+
     return jax.shard_map(body, mesh=mesh3, in_specs=in_specs, out_specs=out_specs, check_vma=False)

time: 155 us -> 155 us (level)
  other arithmetic: 3.11 us -> 7.96 us
  matrix products: 22.2 us -> 17.8 us
    dot_general x1, matrix products: 11.9 us -> 6.77 us  [body(): lax.dot_general(own, ints_own, dims, precision=lax.Precision.HIGH)]
    select_n x0 -> x1, other arithmetic: none -> 4.85 us  [body(): ints_other = jnp.where(first, ints_c1, ints_c0)]
  transfers between devices with their start and end apart: 2 -> 2, of which waited for: 2 -> 1; matrix products, arithmetic and copies ran while one was open for 8% -> 8% of each run, Pallas kernels for 0% -> 0%
where the time goes in v11:
time: 155 us; the launch traced here: 154 us
  waiting for transfers between devices  74.1 us (48%)
  blocking collectives  37.3 us (24%)
  matrix products  17.8 us (11%)
  between operations  13.5 us (9%)
  other arithmetic  7.96 us (5%)
  local copies, waits for them, and re-layouts  2.72 us (2%)
    all_gather x1, waiting for transfers between devices, body(): own = lax.all_gather(amp_t, PLANE, axis=0, tiled=True)  74.1 us
    all_to_all x1, blocking collectives, body(): lax.all_to_all(buf, ('row',) + COL, split_axis=0, concat_axis=0, tiled=True)  37.3 us
    dot_general x1, matrix products, body(): lax.dot_general(other, ints_other, dims, precision=lax.Precision.HIGH)  9.67 us
    dot_general x1, matrix products, body(): lax.dot_general(own, ints_own, dims, precision=lax.Precision.HIGH)  6.77 us
    select_n x1, other arithmetic, body(): ints_other = jnp.where(first, ints_c1, ints_c0)  4.85 us
  transfers between devices with their start and end apart: 2, of which 1 were waited for; matrix products, arithmetic and copies ran while one was open for 8% of the time, Pallas kernels for 0%

profile of v11, /device:TPU:1, one launch (start us, length us, event | category | flops | bytes accessed | tf_op | source)
XLA Modules:
  0.0 154.3 jit_solution(4427289181674020537)
XLA Ops:
  6.5 0.0 copy-start
  6.5 0.0 all-gather.2.cloned.1.call-start
  6.5 0.9 convert_reduce_fusion
  7.5 0.1 mul.47
  7.6 1.1 multiply_bitcast_fusion
  8.7 0.3 copy.19
  9.0 1.0 copy.20
  10.0 0.0 all-gather.2.cloned.1.call-update
  10.0 74.1 %all-gather.2.cloned.1.call-done = f32[2048,1024]{1,0:T(8,128)} async-done(((f32[128,1024]{1,0:T(8,128)}), f32[2048,1024]{1,0:T(8,128)}) %all-gather.2.cloned.1.call-update) | async-done | bytes 8388624 | tf_op jit(solution)/shard_map/all_gather | solution.py:45
  84.2 0.8 collective-permute-start
  85.0 0.8 dynamic-slice_convert_fusion
  85.8 0.1 broadcast_in_dim.4
  85.9 0.1 reshape_reshape.3
  86.0 0.0 slice-start
  86.0 0.1 fusion.7
  86.1 0.0 slice-start.1
  86.1 4.9 %fusion.2 = (f32[16,128,512]{2,1,0:T(8,128)S(1)}, f32[16,128,512]{2,1,0:T(8,128)S(1)}) fusion(f32[16,2,128,512]{3,2,1,0:T(8,128)} %bitcast.58, f32[16,512]{1,0:T(8,128)S(1)} %get-tuple-element.13, f32[16,512]{1,0:T(8,128)S(1)} %get-tuple-element.14, pred[]{:T(512)S(6)} %eq.3), kind=kLoop, calls=%fused_computation.4 | loop fusion | flops 4194304 | bytes 16842752 | tf_op jit(solution)/shard_map/jit(_where)/select_n | solution.py:50
  90.9 0.0 slice-done
  90.9 1.0 slice-done.1
  91.9 6.8 %fusion.8 = f32[1024,512,1]{1,0,2:T(8,128)S(1)} fusion(f32[16,128,1024]{2,1,0:T(8,128)S(1)} %bitcast.67, f32[16,128,512]{2,1,0:T(8,128)S(1)} %get-tuple-element.7), kind=kOutput, calls=%fused_computation.17 | convolution fusion | flops 6442450944 | bytes 14680064 | tf_op jit(solution)/shard_map/dot_general | solution.py:55
  98.7 0.0 collective-permute-done
  98.7 9.7 %fusion.4 = f32[128,8,4,128]{3,1,2,0:T(8,128)S(1)} fusion(f32[1024,512,1]{1,0,2:T(8,128)S(1)} %fusion.8, f32[16,128,1024]{2,1,0:T(8,128)} %bitcast.8, f32[16,128,512]{2,1,0:T(8,128)S(1)} %get-tuple-element.8), kind=kOutput, calls=%fused_computation.7 | convolution fusion | flops 6442975232 | bytes 16777216 | tf_op jit(solution)/shard_map/dot_general | solution.py:55
  108.4 37.3 %all_to_all.5 = f32[128,8,4,128]{3,1,2,0:T(8,128)S(1)} all-to-all(f32[128,8,4,128]{3,1,2,0:T(8,128)S(1)} %fusion.4), channel_id=1, replica_groups=mesh['row'=4,'z'=4,'y'=4,'core'=2] {'row','z','y','core'}, dimensions={0} | all-to-all | bytes 4194304 | tf_op jit(solution)/shard_map/all_to_all | solution.py:60
  145.7 0.2 reduce_sum.9
  145.9 0.1 copy.24
  146.1 0.0 copy-done
  146.1 1.4 fusion.5
  (2 shorter events, 0.0 us)
Async XLA Ops:
  6.5 139.5 %copy-start = (f32[128,128]{1,0:T(8,128)S(1)}, f32[128,128]{1,0:T(8,128)}, u32[]{:S(2)}) copy-start(f32[128,128]{1,0:T(8,128)} %param.7) | copy-start | bytes 196612
  6.5 77.6 %all-gather.2.cloned.1.call-start = ((), (), s32[]{:S(2)}) async-start(), calls=%async_computation.1 | async-start | bytes 8912896 | tf_op jit(solution)/shard_map/all_gather | solution.py:45
  84.2 14.5 %collective-permute-start = (f32[2048,1024]{1,0:T(8,128)}, f32[2048,1024]{1,0:T(8,128)}, u32[]{:S(2)}, u32[]{:S(2)}) collective-permute-start(f32[2048,1024]{1,0:T(8,128)} %all-gather.2.cloned.1.call-done), channel_id=1, source_target_pairs={{0,1},{1,0},{2,3},{3,2},{4,5},{5,4},{6,7},{7,6},{8,9},{9,8},{10,11... | collective-permute-start | bytes 25165832 | tf_op jit(solution)/shard_map/ppermute | solution.py:47
  86.0 5.0 %slice-start = ((s8[8388608]{0:T(1024)(128)(4,1)}), s8[4194304]{0:T(1024)(128)(4,1)S(1)}, s32[]{:S(2)}) async-start(s8[8388608]{0:T(1024)(128)(4,1)} %bitcast.65), calls=%async_computation.2 | async-start | bytes 8388608
  86.1 5.9 %slice-start.1 = ((s8[8388608]{0:T(1024)(128)(4,1)}), s8[4194304]{0:T(1024)(128)(4,1)S(1)}, s32[]{:S(2)}) async-start(s8[8388608]{0:T(1024)(128)(4,1)} %bitcast.65), calls=%async_computation.3 | async-start | bytes 8388608
Sparse Core Ops, SparseCore 0:
  10.2 73.9 all-gather.1

commit v12 on v10

--- a/solution.py
+++ b/solution.py
@@ -3,6 +3,7 @@
 from jax import lax
 from jax.experimental.layout import Layout, with_layout_constraint
 from jax.sharding import Mesh
+
 from jax.sharding import PartitionSpec as P
 
 PLANE = ("z", "y")
@@ -41,17 +42,19 @@
     ints_c0 = ints[:, 0] * masks[:, 0]
     ints_c1 = ints[:, 1] * masks[:, 1]
 
-    own = with_layout_constraint(lax.all_gather(amp_t, PLANE, axis=0, tiled=True), Layout((0, 1)))
-    other = lax.ppermute(own, "core", [(0, 1), (1, 0)])
+    own = lax.all_gather(amp_t, PLANE, axis=0, tiled=True)
+    own = with_layout_constraint(own, Layout((0, 1)))
+    swap = [(0, 1), (1, 0)]
     first = core_id == 0
     ints_own = jnp.where(first, ints_c0, ints_c1)
     ints_other = jnp.where(first, ints_c1, ints_c0)
+    ints_own, ints_other = lax.optimization_barrier((ints_own, ints_other))
+    ints_lent = lax.ppermute(ints_other, "core", swap)
     own = own.reshape(n_zy, k_local, pairs)
-    other = other.reshape(n_zy, k_local, pairs)
     dims = (((0, 1), (0, 1)), ((), ()))
-    partial = lax.dot_general(own, ints_own, dims, precision=lax.Precision.HIGH) + lax.dot_general(
-        other, ints_other, dims, precision=lax.Precision.HIGH
-    )
+    lent_part = lax.dot_general(own, ints_lent, dims, precision=lax.Precision.HIGH)
+    returned = lax.ppermute(lent_part, "core", swap)
+    partial = lax.dot_general(own, ints_own, dims, precision=lax.Precision.HIGH) + returned
 
     buf = partial.reshape(n_row * occ_j, i_local, a_cols, virt)
     recv = lax.all_to_all(buf, ("row",) + COL, split_axis=0, concat_axis=0, tiled=True)
@@ -66,4 +69,5 @@
     mesh3 = Mesh(mesh.devices.reshape(n_row, n_side, n_col // 2 // n_side, 2), ("row",) + COL)
     in_specs = (P(None, ("row",) + COL), P("row", COL), P(), P(), P())
     out_specs = P("row", COL, None, None)
+
     return jax.shard_map(body, mesh=mesh3, in_specs=in_specs, out_specs=out_specs, check_vma=False)

time: 155 us -> 150 us (0.968)
  waiting for transfers between devices: 74.3 us -> 65 us
  other arithmetic: 3.11 us -> 10.3 us
  matrix products: 22.2 us -> 18.3 us
  starting transfers between devices: 0.84 us -> 2.48 us
    all_gather x1, waiting for transfers between devices: 74.1 us -> 58.1 us  [body(): own = lax.all_gather(amp_t, PLANE, axis=0, tiled=True)]
    ppermute x1 -> x2, waiting for transfers between devices: 0.15 us -> 6.92 us  [the longest x1 6.92 us: body(): ints_lent = lax.ppermute(ints_other, 'core', swap)]
    select_n x0 -> x1, other arithmetic: none -> 6.7 us  [body(): ints_other = jnp.where(first, ints_c1, ints_c0)]
    dot_general x1, matrix products: 11.9 us -> 6.8 us  [body(): lax.dot_general(own, ints_own, dims, precision=lax.Precision.HIGH)]
    ppermute x1 -> x2, starting transfers between devices: 0.84 us -> 2.48 us  [the longest x1 1.38 us: body(): ints_lent = lax.ppermute(ints_other, 'core', swap)]
  transfers between devices with their start and end apart: 2 -> 3, of which waited for: 2 -> 2; matrix products, arithmetic and copies ran while one was open for 8% -> 10% of each run, Pallas kernels for 0% -> 0%
where the time goes in v12:
time: 150 us
  waiting for transfers between devices  65 us (43%)
  blocking collectives  37.3 us (25%)
  matrix products  18.3 us (12%)
  between operations  13.5 us (9%)
  other arithmetic  10.3 us (7%)
  local copies, waits for them, and re-layouts  2.83 us (2%)
  starting transfers between devices  2.48 us (2%)
    all_gather x1, waiting for transfers between devices, body(): own = lax.all_gather(amp_t, PLANE, axis=0, tiled=True)  58.1 us
    all_to_all x1, blocking collectives, body(): lax.all_to_all(buf, ('row',) + COL, split_axis=0, concat_axis=0, tiled=True)  37.3 us
    dot_general x1, matrix products, body(): lax.dot_general(own, ints_lent, dims, precision=lax.Precision.HIGH)  10.6 us
    ppermute x1, waiting for transfers between devices, body(): ints_lent = lax.ppermute(ints_other, 'core', swap)  6.92 us
    dot_general x1, matrix products, body(): lax.dot_general(own, ints_own, dims, precision=lax.Precision.HIGH)  6.8 us
    select_n x1, other arithmetic, body(): ints_other = jnp.where(first, ints_c1, ints_c0)  6.7 us
  transfers between devices with their start and end apart: 3, of which 2 were waited for; matrix products, arithmetic and copies ran while one was open for 10% of the time, Pallas kernels for 0%

profile of v12, /device:TPU:1, one launch (start us, length us, event | category | flops | bytes accessed | tf_op | source)
XLA Modules:
  0.0 149.8 jit_solution(14450436348965063303)
XLA Ops:
  6.5 0.0 copy-start
  6.5 0.0 all-gather.2.cloned.1.call-start
  6.5 0.9 convert_reduce_fusion
  7.5 0.1 mul.47
  7.6 1.1 multiply_bitcast_fusion
  8.7 0.3 copy.14
  9.0 1.0 copy.15
  10.0 0.0 all-gather.2.cloned.1.call-update
  10.1 0.8 dynamic-slice_convert_fusion
  10.9 0.1 broadcast_in_dim.4
  11.0 0.1 reshape_reshape.3
  11.0 0.1 fusion.8
  11.1 6.7 %fusion.2 = (f32[16,128,512]{2,1,0:T(8,128)S(1)}, f32[16,128,512]{2,1,0:T(8,128)}) fusion(f32[16,2,128,512]{3,2,1,0:T(8,128)} %bitcast.57, f32[16,512]{1,0:T(8,128)S(1)} %get-tuple-element.13, f32[16,512]{1,0:T(8,128)S(1)} %get-tuple-element.14, pred[]{:T(512)S(6)} %eq.3), kind=kLoop, calls=%fused_computation.4 | loop fusion | flops 4194304 | bytes 16842752 | tf_op jit(solution)/shard_map/jit(_where)/select_n | solution.py:50
  17.8 1.4 collective-permute-start
  19.2 6.9 %collective-permute-done = f32[16,128,512]{2,1,0:T(8,128)} collective-permute-done((f32[16,128,512]{2,1,0:T(8,128)S(1)}, f32[16,128,512]{2,1,0:T(8,128)}, u32[]{:S(2)}, u32[]{:S(2)}) %collective-permute-start) | collective-permute-done | bytes 4194336 | tf_op jit(solution)/shard_map/ppermute | solution.py:52
  26.1 58.1 %all-gather.2.cloned.1.call-done = f32[2048,1024]{1,0:T(8,128)} async-done(((f32[128,1024]{1,0:T(8,128)}), f32[2048,1024]{1,0:T(8,128)}) %all-gather.2.cloned.1.call-update) | async-done | bytes 8388624 | tf_op jit(solution)/shard_map/all_gather | solution.py:45
  84.2 0.0 copy-start.1
  84.2 0.0 copy-start.2
  84.2 10.6 %convolution_bitcast_fusion = f32[1024,512]{1,0:T(8,128)S(1)} fusion(f32[16,128,1024]{2,1,0:T(8,128)} %bitcast.63, f32[16,128,512]{2,1,0:T(8,128)} %collective-permute-done), kind=kOutput, calls=%fused_computation.8 | convolution fusion | flops 6442450944 | bytes 14680064 | tf_op jit(solution)/shard_map/dot_general | solution.py:55
  94.7 1.1 collective-permute-start.1
  95.8 0.0 copy-done.1
  95.8 0.0 copy-done.2
  95.8 6.8 %fusion.9 = f32[1024,512,1]{1,0,2:T(8,128)S(1)} fusion(f32[16,128,1024]{2,1,0:T(8,128)S(1)} %bitcast.64, f32[16,128,512]{2,1,0:T(8,128)S(1)} %copy-done.1), kind=kOutput, calls=%fused_computation.19 | convolution fusion | flops 6442450944 | bytes 14680064 | tf_op jit(solution)/shard_map/dot_general | solution.py:57
  102.7 0.0 collective-permute-done.1
  102.7 0.5 fusion.4
  103.1 37.3 %all_to_all.5 = f32[128,8,4,128]{3,1,2,0:T(8,128)S(1)} all-to-all(f32[128,8,4,128]{3,1,2,0:T(8,128)S(1)} %fusion.4), channel_id=1, replica_groups=mesh['row'=4,'z'=4,'y'=4,'core'=2] {'row','z','y','core'}, dimensions={0} | all-to-all | bytes 4194304 | tf_op jit(solution)/shard_map/all_to_all | solution.py:60
  140.5 0.2 reduce_sum.9
  140.7 0.2 copy.19
  140.9 0.0 copy-done
  140.9 1.0 fusion.5
  141.9 1.0 copy.20
  (1 shorter events, 0.0 us)
Async XLA Ops:
  6.5 134.4 %copy-start = (f32[128,128]{1,0:T(8,128)S(1)}, f32[128,128]{1,0:T(8,128)}, u32[]{:S(2)}) copy-start(f32[128,128]{1,0:T(8,128)} %param.7) | copy-start | bytes 196612
  6.5 77.6 %all-gather.2.cloned.1.call-start = ((), (), s32[]{:S(2)}) async-start(), calls=%async_computation.1 | async-start | bytes 8912896 | tf_op jit(solution)/shard_map/all_gather | solution.py:45
  17.8 8.3 %collective-permute-start = (f32[16,128,512]{2,1,0:T(8,128)S(1)}, f32[16,128,512]{2,1,0:T(8,128)}, u32[]{:S(2)}, u32[]{:S(2)}) collective-permute-start(f32[16,128,512]{2,1,0:T(8,128)S(1)} %get-tuple-element.8), channel_id=1, source_target_pairs={{0,1},{1,0},{2,3},{3,2},{4,5},{5,4},{6,7},{7,6},{8,9},{9,8},{10,11... | collective-permute-start | bytes 12582920 | tf_op jit(solution)/shard_map/ppermute | solution.py:52
  84.2 11.7 %copy-start.1 = (f32[16,128,512]{2,1,0:T(8,128)S(1)}, f32[16,128,512]{2,1,0:T(8,128)}, u32[]{:S(2)}) copy-start(f32[16,128,512]{2,1,0:T(8,128)} %get-tuple-element.7) | copy-start | bytes 12582916
  84.2 11.7 %copy-start.2 = (f32[2048,1024]{1,0:T(8,128)S(1)}, f32[2048,1024]{1,0:T(8,128)}, u32[]{:S(2)}) copy-start(f32[2048,1024]{1,0:T(8,128)} %all-gather.2.cloned.1.call-done) | copy-start | bytes 25165828
  94.7 7.9 %collective-permute-start.1 = (f32[1024,512]{1,0:T(8,128)S(1)}, f32[1024,512]{1,0:T(8,128)S(1)}, u32[]{:S(2)}, u32[]{:S(2)}) collective-permute-start(f32[1024,512]{1,0:T(8,128)S(1)} %convolution_bitcast_fusion), channel_id=1, source_target_pairs={{0,1},{1,0},{2,3},{3,2},{4,5},{5,4},{6,7},{7,6},{8,9},{9,8},{10,11... | collective-permute-start | bytes 6291464 | tf_op jit(solution)/shard_map/ppermute | solution.py:56
Sparse Core Ops, SparseCore 0:
  10.2 73.9 all-gather.1

commit v13 on v12

--- a/solution.py
+++ b/solution.py
@@ -27,7 +27,7 @@
     amp_col = lax.dynamic_slice_in_dim(amp_mask, c_own, 1, axis=1).astype(jnp.float32)
     i_local = occ_i // n_row
     amp_screened = amplitudes.reshape(occ_i, occ_j, k_local) * amp_col[:, :, None]
-    amp_t = amp_screened.reshape(n_row, i_local, occ_j, k_local).transpose(3, 0, 2, 1)
+    amp_t = amp_screened.reshape(n_row, i_local, occ_j, k_local).transpose(3, 2, 0, 1)
     amp_t = with_layout_constraint(amp_t.reshape(k_local, pairs), Layout((0, 1)))
 
     c_rows = virt // n_row
@@ -56,9 +56,9 @@
     returned = lax.ppermute(lent_part, "core", swap)
     partial = lax.dot_general(own, ints_own, dims, precision=lax.Precision.HIGH) + returned
 
-    buf = partial.reshape(n_row * occ_j, i_local, a_cols, virt)
-    recv = lax.all_to_all(buf, ("row",) + COL, split_axis=0, concat_axis=0, tiled=True)
-    summed = recv.reshape(n_row, n_col, i_local, a_cols, virt).sum(axis=0)
+    buf = partial.reshape(occ_j * n_row, i_local, a_cols, virt)
+    recv = lax.all_to_all(buf, COL + ("row",), split_axis=0, concat_axis=0, tiled=True)
+    summed = recv.reshape(n_col, n_row, i_local, a_cols, virt).sum(axis=1)
     block = summed.transpose(1, 0, 2, 3).reshape(i_local, 1, n_col * a_cols, virt)
     return block + jnp.einsum("ac,ijcb->ijab", vv_coupling, block, precision=lax.Precision.HIGHEST)
 

time: 150 us -> 151 us (level)
  no operation moved by 1% of the time
where the time goes in v13:
time: 151 us; the launch traced here: 150 us
  waiting for transfers between devices  65 us (43%)
  blocking collectives  37.9 us (25%)
  matrix products  18.3 us (12%)
  between operations  13.5 us (9%)
  other arithmetic  10.4 us (7%)
  local copies, waits for them, and re-layouts  2.83 us (2%)
  starting transfers between devices  2.48 us (2%)
    all_gather x1, waiting for transfers between devices, body(): own = lax.all_gather(amp_t, PLANE, axis=0, tiled=True)  58.1 us
    all_to_all x1, blocking collectives, body(): lax.all_to_all(buf, COL + ('row',), split_axis=0, concat_axis=0, tiled=True)  37.9 us
    dot_general x1, matrix products, body(): lax.dot_general(own, ints_lent, dims, precision=lax.Precision.HIGH)  10.6 us
    ppermute x1, waiting for transfers between devices, body(): ints_lent = lax.ppermute(ints_other, 'core', swap)  6.92 us
    dot_general x1, matrix products, body(): lax.dot_general(own, ints_own, dims, precision=lax.Precision.HIGH)  6.8 us
    select_n x1, other arithmetic, body(): ints_other = jnp.where(first, ints_c1, ints_c0)  6.7 us
  transfers between devices with their start and end apart: 3, of which 2 were waited for; matrix products, arithmetic and copies ran while one was open for 10% of the time, Pallas kernels for 0%

profile of v13, /device:TPU:1, one launch (start us, length us, event | category | flops | bytes accessed | tf_op | source)
XLA Modules:
  0.0 150.4 jit_solution(11265320542622729001)
XLA Ops:
  6.5 0.0 copy-start
  6.5 0.0 all-gather.2.cloned.1.call-start
  6.5 0.9 convert_reduce_fusion
  7.5 0.1 mul.47
  7.6 1.1 multiply_bitcast_fusion
  8.7 0.3 copy.14
  9.0 1.0 copy.15
  10.0 0.0 all-gather.2.cloned.1.call-update
  10.1 0.8 dynamic-slice_convert_fusion
  10.9 0.1 broadcast_in_dim.4
  11.0 0.1 reshape_reshape.3
  11.0 0.1 fusion.7
  11.1 6.7 %fusion.2 = (f32[16,128,512]{2,1,0:T(8,128)S(1)}, f32[16,128,512]{2,1,0:T(8,128)}) fusion(f32[16,2,128,512]{3,2,1,0:T(8,128)} %bitcast.56, f32[16,512]{1,0:T(8,128)S(1)} %get-tuple-element.13, f32[16,512]{1,0:T(8,128)S(1)} %get-tuple-element.14, pred[]{:T(512)S(6)} %eq.3), kind=kLoop, calls=%fused_computation.4 | loop fusion | flops 4194304 | bytes 16842752 | tf_op jit(solution)/shard_map/jit(_where)/select_n | solution.py:50
  17.8 1.4 collective-permute-start
  19.2 6.9 %collective-permute-done = f32[16,128,512]{2,1,0:T(8,128)} collective-permute-done((f32[16,128,512]{2,1,0:T(8,128)S(1)}, f32[16,128,512]{2,1,0:T(8,128)}, u32[]{:S(2)}, u32[]{:S(2)}) %collective-permute-start) | collective-permute-done | bytes 4194336 | tf_op jit(solution)/shard_map/ppermute | solution.py:52
  26.1 58.1 %all-gather.2.cloned.1.call-done = f32[2048,1024]{1,0:T(8,128)} async-done(((f32[128,1024]{1,0:T(8,128)}), f32[2048,1024]{1,0:T(8,128)}) %all-gather.2.cloned.1.call-update) | async-done | bytes 8388624 | tf_op jit(solution)/shard_map/all_gather | solution.py:45
  84.2 0.0 copy-start.1
  84.2 0.0 copy-start.2
  84.2 10.6 %convolution_bitcast_fusion = f32[1024,512]{1,0:T(8,128)S(1)} fusion(f32[16,128,1024]{2,1,0:T(8,128)} %bitcast.61, f32[16,128,512]{2,1,0:T(8,128)} %collective-permute-done), kind=kOutput, calls=%fused_computation.9 | convolution fusion | flops 6442450944 | bytes 14680064 | tf_op jit(solution)/shard_map/dot_general | solution.py:55
  94.7 1.1 collective-permute-start.1
  95.8 0.0 copy-done.1
  95.8 0.0 copy-done.2
  95.8 6.8 %fusion.8 = f32[1024,512,1]{1,0,2:T(8,128)S(1)} fusion(f32[16,128,1024]{2,1,0:T(8,128)S(1)} %bitcast.62, f32[16,128,512]{2,1,0:T(8,128)S(1)} %copy-done.1), kind=kOutput, calls=%fused_computation.19 | convolution fusion | flops 6442450944 | bytes 14680064 | tf_op jit(solution)/shard_map/dot_general | solution.py:57
  102.6 0.0 collective-permute-done.1
  102.7 0.5 fusion.4
  103.1 37.9 %all_to_all.5 = f32[128,8,4,128]{3,1,2,0:T(8,128)S(1)} all-to-all(f32[128,8,4,128]{3,1,2,0:T(8,128)S(1)} %fusion.4), channel_id=1, replica_groups=mesh['row'=4,'z'=4,'y'=4,'core'=2] {'z','y','core','row'}, dimensions={0} | all-to-all | bytes 4194304 | tf_op jit(solution)/shard_map/all_to_all | solution.py:60
  141.0 0.2 bitcast_reduce_fusion
  141.3 0.2 copy.19
  141.5 0.0 copy-done
  141.5 1.0 convolution_bitcast_fusion.1
  142.5 0.1 add.31
  142.6 1.0 copy.20
  (1 shorter events, 0.0 us)
Async XLA Ops:
  6.5 135.0 %copy-start = (f32[128,128]{1,0:T(8,128)S(1)}, f32[128,128]{1,0:T(8,128)}, u32[]{:S(2)}) copy-start(f32[128,128]{1,0:T(8,128)} %param.7) | copy-start | bytes 196612
  6.5 77.6 %all-gather.2.cloned.1.call-start = ((), (), s32[]{:S(2)}) async-start(), calls=%async_computation.1 | async-start | bytes 8912896 | tf_op jit(solution)/shard_map/all_gather | solution.py:45
  17.8 8.3 %collective-permute-start = (f32[16,128,512]{2,1,0:T(8,128)S(1)}, f32[16,128,512]{2,1,0:T(8,128)}, u32[]{:S(2)}, u32[]{:S(2)}) collective-permute-start(f32[16,128,512]{2,1,0:T(8,128)S(1)} %get-tuple-element.8), channel_id=1, source_target_pairs={{0,1},{1,0},{2,3},{3,2},{4,5},{5,4},{6,7},{7,6},{8,9},{9,8},{10,11... | collective-permute-start | bytes 12582920 | tf_op jit(solution)/shard_map/ppermute | solution.py:52
  84.2 11.7 %copy-start.1 = (f32[16,128,512]{2,1,0:T(8,128)S(1)}, f32[16,128,512]{2,1,0:T(8,128)}, u32[]{:S(2)}) copy-start(f32[16,128,512]{2,1,0:T(8,128)} %get-tuple-element.7) | copy-start | bytes 12582916
  84.2 11.7 %copy-start.2 = (f32[2048,1024]{1,0:T(8,128)S(1)}, f32[2048,1024]{1,0:T(8,128)}, u32[]{:S(2)}) copy-start(f32[2048,1024]{1,0:T(8,128)} %all-gather.2.cloned.1.call-done) | copy-start | bytes 25165828
  94.7 7.9 %collective-permute-start.1 = (f32[1024,512]{1,0:T(8,128)S(1)}, f32[1024,512]{1,0:T(8,128)S(1)}, u32[]{:S(2)}, u32[]{:S(2)}) collective-permute-start(f32[1024,512]{1,0:T(8,128)S(1)} %convolution_bitcast_fusion), channel_id=1, source_target_pairs={{0,1},{1,0},{2,3},{3,2},{4,5},{5,4},{6,7},{7,6},{8,9},{9,8},{10,11... | collective-permute-start | bytes 6291464 | tf_op jit(solution)/shard_map/ppermute | solution.py:56
Sparse Core Ops, SparseCore 0:
  10.2 73.9 all-gather.1

commit v14 on v12

--- a/solution.py
+++ b/solution.py
@@ -60,7 +60,10 @@
     recv = lax.all_to_all(buf, ("row",) + COL, split_axis=0, concat_axis=0, tiled=True)
     summed = recv.reshape(n_row, n_col, i_local, a_cols, virt).sum(axis=0)
     block = summed.transpose(1, 0, 2, 3).reshape(i_local, 1, n_col * a_cols, virt)
-    return block + jnp.einsum("ac,ijcb->ijab", vv_coupling, block, precision=lax.Precision.HIGHEST)
+    row_major = Layout((0, 1, 2, 3))
+    block = with_layout_constraint(block, row_major)
+    out = block + jnp.einsum("ac,ijcb->ijab", vv_coupling, block, precision=lax.Precision.HIGHEST)
+    return with_layout_constraint(out, row_major)
 
 
 def solution(mesh):

time: 150 us -> 149 us (level)
  no operation moved by 1% of the time
where the time goes in v14:
time: 149 us
  waiting for transfers between devices  65 us (44%)
  blocking collectives  37.3 us (25%)
  matrix products  18.8 us (13%)
  between operations  13.5 us (9%)
  other arithmetic  10.3 us (7%)
  starting transfers between devices  2.48 us (2%)
  local copies, waits for them, and re-layouts  1.74 us (1%)
    all_gather x1, waiting for transfers between devices, body(): own = lax.all_gather(amp_t, PLANE, axis=0, tiled=True)  58.1 us
    all_to_all x1, blocking collectives, body(): lax.all_to_all(buf, ('row',) + COL, split_axis=0, concat_axis=0, tiled=True)  37.3 us
    dot_general x1, matrix products, body(): lax.dot_general(own, ints_lent, dims, precision=lax.Precision.HIGH)  10.6 us
    ppermute x1, waiting for transfers between devices, body(): ints_lent = lax.ppermute(ints_other, 'core', swap)  6.92 us
    dot_general x1, matrix products, body(): lax.dot_general(own, ints_own, dims, precision=lax.Precision.HIGH)  6.8 us
    select_n x1, other arithmetic, body(): ints_other = jnp.where(first, ints_c1, ints_c0)  6.7 us
  transfers between devices with their start and end apart: 3, of which 2 were waited for; matrix products, arithmetic and copies ran while one was open for 10% of the time, Pallas kernels for 0%

profile of v14, /device:TPU:1, one launch (start us, length us, event | category | flops | bytes accessed | tf_op | source)
XLA Modules:
  0.0 149.1 jit_solution(7462941147774525917)
XLA Ops:
  6.5 0.0 copy-start
  6.5 0.0 all-gather.2.cloned.1.call-start
  6.5 0.9 convert_reduce_fusion
  7.5 0.1 mul.47
  7.6 1.1 multiply_bitcast_fusion
  8.7 0.3 copy.14
  9.0 1.0 copy.15
  10.0 0.0 all-gather.2.cloned.1.call-update
  10.1 0.8 dynamic-slice_convert_fusion
  10.9 0.1 broadcast_in_dim.4
  11.0 0.1 reshape_reshape.3
  11.0 0.1 fusion.7
  11.1 6.7 %fusion.2 = (f32[16,128,512]{2,1,0:T(8,128)S(1)}, f32[16,128,512]{2,1,0:T(8,128)}) fusion(f32[16,2,128,512]{3,2,1,0:T(8,128)} %bitcast.57, f32[16,512]{1,0:T(8,128)S(1)} %get-tuple-element.13, f32[16,512]{1,0:T(8,128)S(1)} %get-tuple-element.14, pred[]{:T(512)S(6)} %eq.3), kind=kLoop, calls=%fused_computation.4 | loop fusion | flops 4194304 | bytes 16842752 | tf_op jit(solution)/shard_map/jit(_where)/select_n | solution.py:50
  17.8 1.4 collective-permute-start
  19.2 6.9 %collective-permute-done = f32[16,128,512]{2,1,0:T(8,128)} collective-permute-done((f32[16,128,512]{2,1,0:T(8,128)S(1)}, f32[16,128,512]{2,1,0:T(8,128)}, u32[]{:S(2)}, u32[]{:S(2)}) %collective-permute-start) | collective-permute-done | bytes 4194336 | tf_op jit(solution)/shard_map/ppermute | solution.py:52
  26.1 58.1 %all-gather.2.cloned.1.call-done = f32[2048,1024]{1,0:T(8,128)} async-done(((f32[128,1024]{1,0:T(8,128)}), f32[2048,1024]{1,0:T(8,128)}) %all-gather.2.cloned.1.call-update) | async-done | bytes 8388624 | tf_op jit(solution)/shard_map/all_gather | solution.py:45
  84.2 0.0 copy-start.1
  84.2 0.0 copy-start.2
  84.2 10.6 %convolution_bitcast_fusion = f32[1024,512]{1,0:T(8,128)S(1)} fusion(f32[16,128,1024]{2,1,0:T(8,128)} %bitcast.64, f32[16,128,512]{2,1,0:T(8,128)} %collective-permute-done), kind=kOutput, calls=%fused_computation.8 | convolution fusion | flops 6442450944 | bytes 14680064 | tf_op jit(solution)/shard_map/dot_general | solution.py:55
  94.7 1.1 collective-permute-start.1
  95.8 0.0 copy-done.1
  95.8 0.0 copy-done.2
  95.8 6.8 %fusion.8 = f32[1024,512,1]{1,0,2:T(8,128)S(1)} fusion(f32[16,128,1024]{2,1,0:T(8,128)S(1)} %bitcast.65, f32[16,128,512]{2,1,0:T(8,128)S(1)} %copy-done.1), kind=kOutput, calls=%fused_computation.18 | convolution fusion | flops 6442450944 | bytes 14680064 | tf_op jit(solution)/shard_map/dot_general | solution.py:57
  102.7 0.0 collective-permute-done.1
  102.7 0.5 fusion.4
  103.1 37.3 %all_to_all.5 = f32[128,8,4,128]{3,1,2,0:T(8,128)S(1)} all-to-all(f32[128,8,4,128]{3,1,2,0:T(8,128)S(1)} %fusion.4), channel_id=1, replica_groups=mesh['row'=4,'z'=4,'y'=4,'core'=2] {'row','z','y','core'}, dimensions={0} | all-to-all | bytes 4194304 | tf_op jit(solution)/shard_map/all_to_all | solution.py:60
  140.5 0.2 reduce_sum.9
  140.7 0.1 copy.18
  140.8 0.0 copy-done
  140.9 1.4 fusion.5
  (1 shorter events, 0.0 us)
Async XLA Ops:
  6.5 134.3 %copy-start = (f32[128,128]{1,0:T(8,128)S(1)}, f32[128,128]{1,0:T(8,128)}, u32[]{:S(2)}) copy-start(f32[128,128]{1,0:T(8,128)} %param.7) | copy-start | bytes 196612
  6.5 77.6 %all-gather.2.cloned.1.call-start = ((), (), s32[]{:S(2)}) async-start(), calls=%async_computation.1 | async-start | bytes 8912896 | tf_op jit(solution)/shard_map/all_gather | solution.py:45
  17.8 8.3 %collective-permute-start = (f32[16,128,512]{2,1,0:T(8,128)S(1)}, f32[16,128,512]{2,1,0:T(8,128)}, u32[]{:S(2)}, u32[]{:S(2)}) collective-permute-start(f32[16,128,512]{2,1,0:T(8,128)S(1)} %get-tuple-element.8), channel_id=1, source_target_pairs={{0,1},{1,0},{2,3},{3,2},{4,5},{5,4},{6,7},{7,6},{8,9},{9,8},{10,11... | collective-permute-start | bytes 12582920 | tf_op jit(solution)/shard_map/ppermute | solution.py:52
  84.2 11.7 %copy-start.1 = (f32[16,128,512]{2,1,0:T(8,128)S(1)}, f32[16,128,512]{2,1,0:T(8,128)}, u32[]{:S(2)}) copy-start(f32[16,128,512]{2,1,0:T(8,128)} %get-tuple-element.7) | copy-start | bytes 12582916
  84.2 11.7 %copy-start.2 = (f32[2048,1024]{1,0:T(8,128)S(1)}, f32[2048,1024]{1,0:T(8,128)}, u32[]{:S(2)}) copy-start(f32[2048,1024]{1,0:T(8,128)} %all-gather.2.cloned.1.call-done) | copy-start | bytes 25165828
  94.7 7.9 %collective-permute-start.1 = (f32[1024,512]{1,0:T(8,128)S(1)}, f32[1024,512]{1,0:T(8,128)S(1)}, u32[]{:S(2)}, u32[]{:S(2)}) collective-permute-start(f32[1024,512]{1,0:T(8,128)S(1)} %convolution_bitcast_fusion), channel_id=1, source_target_pairs={{0,1},{1,0},{2,3},{3,2},{4,5},{5,4},{6,7},{7,6},{8,9},{9,8},{10,11... | collective-permute-start | bytes 6291464 | tf_op jit(solution)/shard_map/ppermute | solution.py:56
Sparse Core Ops, SparseCore 0:
  10.2 73.9 all-gather.1
